TPU v7x, 32 devices: a whole 2x2x4 slice. The times are simulated.
32 devices in a mesh: band: 4 (over y, core), space: 8 (over z, x).
Axes of the slice: x: 2, y: 2, z: 4, core: 2. Of those that a mesh axis runs over, the one named last changes fastest.
Arguments:
- states: float32 [256, 48, 1024], P('band', 'space'), may hold values from -6 to 6
- patch_ids: int32 [48, 32], P('space'), may hold values from 0 to 63
- metric_table: float32 [64, 96], replicated, may hold values from 0.5 to 2
- potential: float32 [48, 1024], P('space'), may hold values from -3 to 0
Outputs:
- orthonormal: float32 [256, 48, 1024], P(None, 'space', 'band')
All inputs are finite; a program needn't handle non-finite values.
Results may differ from a plain program's by a relative error of at most 0.00014.
Values sent between devices are 32-bit elements; how exact they have to be, the bound alone decides.
A program may use at most 64 MiB of HBM per device.

v0:
```python
import jax
import jax.numpy as jnp
from jax import lax
from jax.sharding import PartitionSpec as P

DEGREE = 3
NY = 32
NZ = 32


CENTRE = 8.5
HALF_WIDTH = 7.5
OFFSETS = (-2, -1, 0, 1, 2)
WEIGHTS = (-1.0 / 12.0, 4.0 / 3.0, -2.5, 4.0 / 3.0, -1.0 / 12.0)


def with_halo(cells, sides, width):
    for axis, dim in sides:
        count = lax.axis_size(axis)
        ends = count - 1
        head = lax.slice_in_dim(cells, 0, width, axis=dim)
        tail = lax.slice_in_dim(cells, cells.shape[dim] - width, cells.shape[dim], axis=dim)
        cells = jnp.concatenate(
            [
                lax.ppermute(tail, axis, [(i, (i + 1) % count) for i in range(ends)]),
                cells,
                lax.ppermute(head, axis, [((i + 1) % count, i) for i in range(ends)]),
            ],
            axis=dim,
        )
    return cells


def swapped(value, axis, bit):
    mask = 2**bit
    pairs = [(source, source ^ mask) for source in range(lax.axis_size(axis))]
    return lax.ppermute(value, axis, pairs)


def apply_ham(extended, potential, metric, z_weights):
    planes = extended.shape[1] - 4
    plane_cells = extended.shape[2]
    block = extended[:, 2 : 2 + planes, :]
    row_pad = 2 * NZ
    padded = jnp.pad(block, ((0, 0), (0, 0), (row_pad, row_pad)))
    x_term = WEIGHTS[0] * extended[:, 2 + OFFSETS[0] : 2 + OFFSETS[0] + planes, :]
    y_term = (
        WEIGHTS[0]
        * padded[:, :, row_pad + OFFSETS[0] * NZ : row_pad + OFFSETS[0] * NZ + plane_cells]
    )
    z_term = z_weights[0] * padded[:, :, row_pad + OFFSETS[0] : row_pad + OFFSETS[0] + plane_cells]
    for position in range(1, 5):
        offset = OFFSETS[position]
        weight = WEIGHTS[position]
        x_term = x_term + weight * extended[:, 2 + offset : 2 + offset + planes, :]
        y_term = (
            y_term
            + weight * padded[:, :, row_pad + offset * NZ : row_pad + offset * NZ + plane_cells]
        )
        z_term = (
            z_term
            + z_weights[position] * padded[:, :, row_pad + offset : row_pad + offset + plane_cells]
        )
    kinetic = metric[0] * x_term + metric[1] * y_term + metric[2] * z_term
    return potential * block - 0.5 * kinetic


def on_device(states, patch_ids, metric_table, potential):
    planes = states.shape[1]
    plane_cells = states.shape[2]
    one_hot = (patch_ids[:, :, None] == jnp.arange(metric_table.shape[0], dtype=jnp.int32)).astype(
        jnp.float32
    )
    looked = jnp.einsum("xyp,pm->xym", one_hot, metric_table, precision=lax.Precision.HIGHEST)
    metric = looked.reshape(planes, NY, 3, NZ).transpose(2, 0, 1, 3).reshape(3, planes, plane_cells)
    z_index = jnp.arange(plane_cells, dtype=jnp.int32) % NZ
    z_weights = [
        WEIGHTS[position]
        * ((z_index + OFFSETS[position] >= 0) & (z_index + OFFSETS[position] < NZ)).astype(
            jnp.float32
        )
        for position in range(5)
    ]

    def step_ham(block):
        extended = with_halo(block, (("space", 1),), 2)
        return apply_ham(extended, potential, metric, z_weights)

    applied = step_ham(states)
    earlier = states
    current = (applied - CENTRE * states) / HALF_WIDTH
    for degree_step in range(DEGREE - 1):
        applied = step_ham(current)
        following = 2.0 * (applied - CENTRE * current) / HALF_WIDTH - earlier
        earlier = current
        current = following
    regrouped = lax.all_to_all(current, "band", split_axis=2, concat_axis=0, tiled=True)
    all_states = regrouped.shape[0]
    flat = regrouped.reshape(all_states, -1)
    cell_total = planes * plane_cells * lax.axis_size("space")
    local_gram = jnp.dot(
        flat, flat.T, precision=lax.Precision.HIGHEST, preferred_element_type=jnp.float32
    )
    device_index = lax.axis_index(("band", "space"))
    levels = lax.axis_size(("band", "space")).bit_length() - 1
    vector = local_gram.reshape(-1)
    for level in range(levels):
        bit = levels - 1 - level
        half = vector.shape[0] // 2
        upper_side = device_index >> bit & 1 == 1
        kept = jnp.where(upper_side, vector[half:], vector[:half])
        sending = jnp.where(upper_side, vector[:half], vector[half:])
        vector = kept + swapped(sending, ("band", "space"), bit)
    for level in range(levels):
        bit = level
        upper_side = device_index >> bit & 1 == 1
        received = swapped(vector, ("band", "space"), bit)
        vector = jnp.where(
            upper_side, jnp.concatenate([received, vector]), jnp.concatenate([vector, received])
        )
    gram = vector.reshape(all_states, all_states) / cell_total
    factor = jnp.linalg.cholesky(gram)
    result = lax.linalg.triangular_solve(factor, flat, left_side=True, lower=True)
    return result.reshape(all_states, planes, regrouped.shape[2])


def solution(mesh):
    return jax.shard_map(
        on_device,
        mesh=mesh,
        in_specs=(P("band", "space", None), P("space", None), P(), P("space", None)),
        out_specs=P(None, "space", "band"),
        check_vma=False,
    )
```

profile of v0, /device:TPU:0, one launch (start us, length us, event | category | flops | bytes accessed | tf_op | source)
XLA Modules:
  0.0 248.5 jit_solution(1068636462713036321)
XLA Ops:
  0.0 2.3 fusion.143
  2.3 5.0 %collective-permute-start = (f32[64,2,1024]{2,0,1:T(8,128)}, f32[64,2,1024]{2,0,1:T(8,128)S(1)}, u32[]{:S(2)}, u32[]{:S(2)}) collective-permute-start(f32[64,2,1024]{2,0,1:T(8,128)} %get-tuple-element.36), channel_id=1, source_target_pairs={{0,1},{1,2},{2,3},{3,4},{4,5},{5,6},{6,7},{8,9},{9,10},{10,11},{11... | collective-permute-start | bytes 1572872 | tf_op jit(solution)/shard_map/ppermute | solution.py:25
  7.3 1.3 collective-permute-start.1
  9.1 0.8 slice_reduce_fusion.2
  10.3 19.7 %collective-permute-done = f32[64,2,1024]{2,0,1:T(8,128)S(1)} collective-permute-done((f32[64,2,1024]{2,0,1:T(8,128)}, f32[64,2,1024]{2,0,1:T(8,128)S(1)}, u32[]{:S(2)}, u32[]{:S(2)}) %collective-permute-start) | collective-permute-done | bytes 524320 | tf_op jit(solution)/shard_map/ppermute | solution.py:25
  30.8 3.6 %broadcast_multiply_fusion = (f32[64,6,1024]{2,0,1:T(8,128)S(1)}, f32[64,6,1024]{2,0,1:T(8,128)S(1)}) fusion(f32[64,6,1024]{2,0,1:T(8,128)S(1)} %copy-done.1, f32[1024]{0:T(1024)S(1)} %get-tuple-element.48, f32[1024]{0:T(1024)S(1)} %get-tuple-element.49, f32[1024]{0:T(1024)S(1)} %fusion.136, f32[1024]{0:T(1024)S(1)} %get-tuple-element.50, ...), kind=kLoop, calls=%fused_computation.145 | loop fusion | flops 14548992 | bytes 11128832 | tf_op jit(solution)/shard_map/div | solution.py:91
  34.5 4.3 %collective-permute-start.2 = (f32[64,2,1024]{2,0,1:T(8,128)S(1)}, f32[64,2,1024]{2,0,1:T(8,128)S(1)}, u32[]{:S(2)}, u32[]{:S(2)}) collective-permute-start(f32[64,2,1024]{2,0,1:T(8,128)S(1)} %get-tuple-element.32), channel_id=1, source_target_pairs={{0,1},{1,2},{2,3},{3,4},{4,5},{5,6},{6,7},{8,9},{9,10},{10,11},{11... | collective-permute-start | bytes 1572872 | tf_op jit(solution)/shard_map/ppermute | solution.py:25
  38.8 1.3 collective-permute-start.3
  40.1 20.2 %collective-permute-done.2 = f32[64,2,1024]{2,0,1:T(8,128)S(1)} collective-permute-done((f32[64,2,1024]{2,0,1:T(8,128)S(1)}, f32[64,2,1024]{2,0,1:T(8,128)S(1)}, u32[]{:S(2)}, u32[]{:S(2)}) %collective-permute-start.2) | collective-permute-done | bytes 524320 | tf_op jit(solution)/shard_map/ppermute | solution.py:25
  60.3 3.8 %fusion.35 = f32[64,6,1024]{2,0,1:T(8,128)S(1)} fusion(f32[64,6,1024]{2,0,1:T(8,128)S(1)} %copy-done.1, f32[64,6,1024]{2,0,1:T(8,128)S(1)} %get-tuple-element.24, f32[64,2,1024]{2,0,1:T(8,128)S(1)} %collective-permute-done.3, f32[64,2,1024]{2,0,1:T(8,128)S(1)} %collective-permute-done.2, f32[64,6,1024]{2,0,1:T(8,128)S(1)} %get-tuple-element.25, ...), kind=kLoop, calls=%fused_computation.70 | loop fusion | flops 16515072 | bytes 7458816 | tf_op jit(solution)/shard_map/sub | solution.py:94
  64.3 4.4 %collective-permute-start.4 = (f32[64,2,1024]{2,0,1:T(8,128)S(1)}, f32[64,2,1024]{2,0,1:T(8,128)S(1)}, u32[]{:S(2)}, u32[]{:S(2)}) collective-permute-start(f32[64,2,1024]{2,0,1:T(8,128)S(1)} %get-tuple-element.30), channel_id=1, source_target_pairs={{0,1},{1,2},{2,3},{3,4},{4,5},{5,6},{6,7},{8,9},{9,10},{10,11},{11... | collective-permute-start | bytes 1572872 | tf_op jit(solution)/shard_map/ppermute | solution.py:25
  68.7 1.3 collective-permute-start.5
  70.0 19.4 %collective-permute-done.4 = f32[64,2,1024]{2,0,1:T(8,128)S(1)} collective-permute-done((f32[64,2,1024]{2,0,1:T(8,128)S(1)}, f32[64,2,1024]{2,0,1:T(8,128)S(1)}, u32[]{:S(2)}, u32[]{:S(2)}) %collective-permute-start.4) | collective-permute-done | bytes 524320 | tf_op jit(solution)/shard_map/ppermute | solution.py:25
  89.3 3.8 %fusion.60 = f32[64,6,1024]{2,0,1:T(8,128)S(1)} fusion(f32[64,6,1024]{2,0,1:T(8,128)S(1)} %fusion.35, f32[64,2,1024]{2,0,1:T(8,128)S(1)} %collective-permute-done.5, f32[64,2,1024]{2,0,1:T(8,128)S(1)} %collective-permute-done.4, f32[64,6,1024]{2,0,1:T(8,128)S(1)} %get-tuple-element.25, f32[1024]{0:T(1024)S(1)} %get-tuple-element.48, ...), kind=kLoop, calls=%fused_computation.95 | loop fusion | flops 16908288 | bytes 5885952 | tf_op jit(solution)/shard_map/sub | solution.py:94
  93.1 2.7 %copy.48 = f32[64,6,1024]{0,1,2:T(8,128)} copy(f32[64,6,1024]{2,0,1:T(8,128)S(1)} %fusion.60) | data formatting | bytes 3145728 | tf_op jit(solution)/shard_map/sub | solution.py:94
  95.9 5.1 %reshape.143 = f32[4,1,98304]{2,1,0:T(1,128)} reshape(f32[1024,6,64]{2,1,0:T(8,128)} %bitcast.60) | data formatting | bytes 3145728
  101.0 3.7 %all-to-all-start = ((f32[4,1,98304]{2,1,0:T(1,128)}), f32[4,1,98304]{2,1,0:T(1,128)S(1)}, u32[]{:S(2)}, u32[]{:S(2)}) async-start(f32[4,1,98304]{2,1,0:T(1,128)} %reshape.143), calls=%async_computation | async-start | bytes 3145728 | tf_op jit(solution)/shard_map/all_to_all | solution.py:97
  104.7 19.8 %all-to-all-done = f32[4,1,98304]{2,1,0:T(1,128)S(1)} async-done(((f32[4,1,98304]{2,1,0:T(1,128)}), f32[4,1,98304]{2,1,0:T(1,128)S(1)}, u32[]{:S(2)}, u32[]{:S(2)}) %all-to-all-start) | async-done | bytes 1572896 | tf_op jit(solution)/shard_map/all_to_all | solution.py:97
  125.1 5.2 %reduce.24 = f32[4,98304]{1,0:T(4,128)S(1)} reduce(f32[4,1,98304]{2,1,0:T(1,128)S(1)} %all-to-all-done, f32[]{:T(128)} %broadcast.404), dimensions={1}, to_apply=%all_to_all.11.reduce_sub_computation | reduce | bytes 3145732 | tf_op jit(solution)/shard_map/all_to_all | solution.py:97
  130.3 3.6 %reshape.144 = f32[1024,6,64]{2,1,0:T(8,128)} reshape(f32[4,98304]{1,0:T(4,128)S(1)} %reduce.24) | data formatting | bytes 3145728
  133.9 3.3 %copy.49 = f32[64,6,4,256]{3,1,0,2:T(8,128)S(1)} copy(f32[64,6,4,256]{0,1,3,2:T(8,128)} %bitcast.61) | data formatting | bytes 3145728 | tf_op jit(solution)/shard_map/all_to_all | solution.py:97
  137.9 1.4 fusion.144
  140.0 4.5 %collective-permute-done.6 = f32[32768]{0:T(1024)S(1)} collective-permute-done((f32[32768]{0:T(1024)S(1)}, f32[32768]{0:T(1024)S(1)}, u32[]{:S(2)}, u32[]{:S(2)}) %collective-permute-start.6) | collective-permute-done | bytes 131104 | tf_op jit(solution)/shard_map/ppermute | solution.py:37
  144.6 1.2 collective-permute-done.7
  145.8 8.5 %collective-permute-start.8 = (f32[8192]{0:T(1024)S(1)}, f32[8192]{0:T(1024)S(1)}, u32[]{:S(2)}, u32[]{:S(2)}) collective-permute-start(f32[8192]{0:T(1024)S(1)} %slice_select_fusion.1), channel_id=1, source_target_pairs={{0,4},{1,5},{2,6},{3,7},{4,0},{5,1},{6,2},{7,3},{8,12},{9,13},{10,... | collective-permute-start | bytes 98312 | tf_op jit(solution)/shard_map/ppermute | solution.py:37
  154.4 1.9 collective-permute-done.8
  156.3 2.0 collective-permute-start.9
  158.3 1.8 collective-permute-done.9
  160.2 3.6 %collective-permute-done.10 = f32[2048]{0:T(1024)S(1)} collective-permute-done((f32[2048]{0:T(1024)S(1)}, f32[2048]{0:T(1024)S(1)}, u32[]{:S(2)}, u32[]{:S(2)}) %collective-permute-start.10) | collective-permute-done | bytes 8224 | tf_op jit(solution)/shard_map/ppermute | solution.py:37
  163.9 3.6 %collective-permute-done.11 = f32[2048]{0:T(1024)S(1)} collective-permute-done((f32[2048]{0:T(1024)S(1)}, f32[2048]{0:T(1024)S(1)}, u32[]{:S(2)}, u32[]{:S(2)}) %collective-permute-start.11) | collective-permute-done | bytes 8224 | tf_op jit(solution)/shard_map/ppermute | solution.py:37
  167.5 1.9 collective-permute-start.12
  170.1 1.1 collective-permute-done.12
  171.2 2.9 %collective-permute-start.13 = (f32[8192]{0:T(1024)S(1)}, f32[8192]{0:T(1024)S(1)}, u32[]{:S(2)}, u32[]{:S(2)}) collective-permute-start(f32[8192]{0:T(1024)S(1)} %maximum_select_fusion.5), channel_id=1, source_target_pairs={{0,4},{1,5},{2,6},{3,7},{4,0},{5,1},{6,2},{7,3},{8,12},{9,13},{10,... | collective-permute-start | bytes 98312 | tf_op jit(solution)/shard_map/ppermute | solution.py:37
  174.4 1.7 collective-permute-done.13
  176.3 1.1 collective-permute-done.14
  178.4 4.6 %collective-permute-done.15 = f32[32768]{0:T(1024)S(1)} collective-permute-done((f32[32768]{0:T(1024)S(1)}, f32[32768]{0:T(1024)S(1)}, u32[]{:S(2)}, u32[]{:S(2)}) %collective-permute-start.15) | collective-permute-done | bytes 131104 | tf_op jit(solution)/shard_map/ppermute | solution.py:37
  183.4 11.7 %cholesky.50 = f32[128,128]{1,0:T(8,128)S(1)} custom-call(f32[128,128]{1,0:T(8,128)S(1)} %cholesky.118), custom_call_target="Cholesky" | custom-call | tf_op jit(solution)/shard_map/jit(cholesky)/cholesky | solution.py:122
  195.2 9.8 %custom-call.14 = f32[1,128,128]{1,2,0:T(8,128)S(1)} custom-call(f32[1,128,128]{2,1,0:T(8,128)S(1)} %get-tuple-element.43), custom_call_target="InvertDiagBlocksLowerTriangular" | custom-call | tf_op jit(solution)/shard_map/jit(cholesky)/cholesky | solution.py:122
  205.5 12.0 %cholesky.105 = f32[128,128]{1,0:T(8,128)S(1)} custom-call(f32[128,128]{1,0:T(8,128)S(1)} %convolution_subtract_fusion.1), custom_call_target="Cholesky" | custom-call | tf_op jit(solution)/shard_map/jit(cholesky)/cholesky | solution.py:122
  217.4 0.7 compare_reduce_fusion
  220.2 4.0 %while.1 = (s32[]{:T(128)}, f32[256,256]{1,0:T(8,128)S(1)}, s32[2,2]{1,0:T(2,128)S(1)}, f32[2,128,128]{2,1,0:T(8,128)S(1)}, s32[]{:T(128)}) while((s32[]{:T(128)}, f32[256,256]{1,0:T(8,128)S(1)}, s32[2,2]{1,0:T(2,128)S(1)}, f32[2,128,128]{2,1,0:T(8,128)S(1)}, s32[]{:T(128)}) %tuple.34), condition=%wide.while_cond, body=%wide.while_body.sunk | while | flops 2 | bytes 131181 | solution.py:123
  220.8 1.3 bitcast_dynamic-update-slice_fusion.2
  222.8 1.3 bitcast_dynamic-update-slice_fusion.2
  224.2 19.7 %custom-call.15 = f32[2,128,128]{1,2,0:T(8,128)S(1)} custom-call(f32[2,128,128]{2,1,0:T(8,128)S(1)} %get-tuple-element.12), custom_call_target="InvertDiagBlocksLowerTriangular" | custom-call | tf_op jit(solution)/shard_map/triangular_solve | solution.py:123
  243.8 0.8 fusion.105
  244.7 0.8 convolution_subtract_fusion
  245.5 0.8 fusion.104
  246.9 1.6 copy.60
  (87 shorter events, 9.4 us)
Async XLA Ops:
  0.0 8.6 %copy-start = (f32[64,96]{1,0:T(8,128)S(1)}, f32[64,96]{1,0:T(8,128)}, u32[]{:S(2)}) copy-start(f32[64,96]{1,0:T(8,128)} %param.6) | copy-start | bytes 73732
  0.0 8.6 %copy-start.3 = (s32[6,32]{1,0:T(8,128)S(1)}, s32[6,32]{1,0:T(8,128)}, u32[]{:S(2)}) copy-start(s32[6,32]{1,0:T(8,128)} %param.5) | copy-start | bytes 2308
  2.3 27.8 %copy-start.1 = (f32[64,6,1024]{2,0,1:T(8,128)S(1)}, f32[64,6,1024]{2,0,1:T(8,128)}, u32[]{:S(2)}) copy-start(f32[64,6,1024]{2,0,1:T(8,128)} %param.4) | copy-start | bytes 4718596
  2.3 27.7 %collective-permute-start = (f32[64,2,1024]{2,0,1:T(8,128)}, f32[64,2,1024]{2,0,1:T(8,128)S(1)}, u32[]{:S(2)}, u32[]{:S(2)}) collective-permute-start(f32[64,2,1024]{2,0,1:T(8,128)} %get-tuple-element.36), channel_id=1, source_target_pairs={{0,1},{1,2},{2,3},{3,4},{4,5},{5,6},{6,7},{8,9},{9,10},{10,11},{11... | collective-permute-start | bytes 1572872 | tf_op jit(solution)/shard_map/ppermute | solution.py:25
  7.3 23.0 %collective-permute-start.1 = (f32[64,2,1024]{2,0,1:T(8,128)}, f32[64,2,1024]{2,0,1:T(8,128)S(1)}, u32[]{:S(2)}, u32[]{:S(2)}) collective-permute-start(f32[64,2,1024]{2,0,1:T(8,128)} %get-tuple-element.37), channel_id=1, source_target_pairs={{1,0},{2,1},{3,2},{4,3},{5,4},{6,5},{7,6},{9,8},{10,9},{11,10},{12... | collective-permute-start | bytes 1572872 | tf_op jit(solution)/shard_map/ppermute | solution.py:27
  30.1 0.8 copy-start.2
  34.5 25.8 %collective-permute-start.2 = (f32[64,2,1024]{2,0,1:T(8,128)S(1)}, f32[64,2,1024]{2,0,1:T(8,128)S(1)}, u32[]{:S(2)}, u32[]{:S(2)}) collective-permute-start(f32[64,2,1024]{2,0,1:T(8,128)S(1)} %get-tuple-element.32), channel_id=1, source_target_pairs={{0,1},{1,2},{2,3},{3,4},{4,5},{5,6},{6,7},{8,9},{9,10},{10,11},{11... | collective-permute-start | bytes 1572872 | tf_op jit(solution)/shard_map/ppermute | solution.py:25
  38.8 21.5 %collective-permute-start.3 = (f32[64,2,1024]{2,0,1:T(8,128)S(1)}, f32[64,2,1024]{2,0,1:T(8,128)S(1)}, u32[]{:S(2)}, u32[]{:S(2)}) collective-permute-start(f32[64,2,1024]{2,0,1:T(8,128)S(1)} %get-tuple-element.33), channel_id=1, source_target_pairs={{1,0},{2,1},{3,2},{4,3},{5,4},{6,5},{7,6},{9,8},{10,9},{11,10},{12... | collective-permute-start | bytes 1572872 | tf_op jit(solution)/shard_map/ppermute | solution.py:27
  64.3 25.1 %collective-permute-start.4 = (f32[64,2,1024]{2,0,1:T(8,128)S(1)}, f32[64,2,1024]{2,0,1:T(8,128)S(1)}, u32[]{:S(2)}, u32[]{:S(2)}) collective-permute-start(f32[64,2,1024]{2,0,1:T(8,128)S(1)} %get-tuple-element.30), channel_id=1, source_target_pairs={{0,1},{1,2},{2,3},{3,4},{4,5},{5,6},{6,7},{8,9},{9,10},{10,11},{11... | collective-permute-start | bytes 1572872 | tf_op jit(solution)/shard_map/ppermute | solution.py:25
  68.7 20.7 %collective-permute-start.5 = (f32[64,2,1024]{2,0,1:T(8,128)S(1)}, f32[64,2,1024]{2,0,1:T(8,128)S(1)}, u32[]{:S(2)}, u32[]{:S(2)}) collective-permute-start(f32[64,2,1024]{2,0,1:T(8,128)S(1)} %get-tuple-element.31), channel_id=1, source_target_pairs={{1,0},{2,1},{3,2},{4,3},{5,4},{6,5},{7,6},{9,8},{10,9},{11,10},{12... | collective-permute-start | bytes 1572872 | tf_op jit(solution)/shard_map/ppermute | solution.py:27
  101.0 23.6 %all-to-all-start = ((f32[4,1,98304]{2,1,0:T(1,128)}), f32[4,1,98304]{2,1,0:T(1,128)S(1)}, u32[]{:S(2)}, u32[]{:S(2)}) async-start(f32[4,1,98304]{2,1,0:T(1,128)} %reshape.143), calls=%async_computation | async-start | bytes 3145728 | tf_op jit(solution)/shard_map/all_to_all | solution.py:97
  139.4 5.0 %collective-permute-start.6 = (f32[32768]{0:T(1024)S(1)}, f32[32768]{0:T(1024)S(1)}, u32[]{:S(2)}, u32[]{:S(2)}) collective-permute-start(f32[32768]{0:T(1024)S(1)} %bitcast.70), channel_id=1, source_target_pairs={{0,16},{1,17},{2,18},{3,19},{4,20},{5,21},{6,22},{7,23},{8,24},{9,... | collective-permute-start | bytes 393224 | tf_op jit(solution)/shard_map/ppermute | solution.py:37
  144.5 1.3 collective-permute-start.7
  145.8 10.4 %collective-permute-start.8 = (f32[8192]{0:T(1024)S(1)}, f32[8192]{0:T(1024)S(1)}, u32[]{:S(2)}, u32[]{:S(2)}) collective-permute-start(f32[8192]{0:T(1024)S(1)} %slice_select_fusion.1), channel_id=1, source_target_pairs={{0,4},{1,5},{2,6},{3,7},{4,0},{5,1},{6,2},{7,3},{8,12},{9,13},{10,... | collective-permute-start | bytes 98312 | tf_op jit(solution)/shard_map/ppermute | solution.py:37
  156.3 3.8 %collective-permute-start.9 = (f32[4096]{0:T(1024)S(1)}, f32[4096]{0:T(1024)S(1)}, u32[]{:S(2)}, u32[]{:S(2)}) collective-permute-start(f32[4096]{0:T(1024)S(1)} %slice_select_fusion.2), channel_id=1, source_target_pairs={{0,2},{1,3},{2,0},{3,1},{4,6},{5,7},{6,4},{7,5},{8,10},{9,11},{10,... | collective-permute-start | bytes 49160 | tf_op jit(solution)/shard_map/ppermute | solution.py:37
  160.1 3.7 %collective-permute-start.10 = (f32[2048]{0:T(1024)S(1)}, f32[2048]{0:T(1024)S(1)}, u32[]{:S(2)}, u32[]{:S(2)}) collective-permute-start(f32[2048]{0:T(1024)S(1)} %slice_select_fusion.3), channel_id=1, source_target_pairs={{0,1},{1,0},{2,3},{3,2},{4,5},{5,4},{6,7},{7,6},{8,9},{9,8},{10,11... | collective-permute-start | bytes 24584 | tf_op jit(solution)/shard_map/ppermute | solution.py:37
  163.8 3.7 %collective-permute-start.11 = (f32[2048]{0:T(1024)S(1)}, f32[2048]{0:T(1024)S(1)}, u32[]{:S(2)}, u32[]{:S(2)}) collective-permute-start(f32[2048]{0:T(1024)S(1)} %select_add_fusion.3), channel_id=1, source_target_pairs={{0,1},{1,0},{2,3},{3,2},{4,5},{5,4},{6,7},{7,6},{8,9},{9,8},{10,11... | collective-permute-start | bytes 24584 | tf_op jit(solution)/shard_map/ppermute | solution.py:37
  167.5 3.7 %collective-permute-start.12 = (f32[4096]{0:T(1024)S(1)}, f32[4096]{0:T(1024)S(1)}, u32[]{:S(2)}, u32[]{:S(2)}) collective-permute-start(f32[4096]{0:T(1024)S(1)} %maximum_select_fusion.6), channel_id=1, source_target_pairs={{0,2},{1,3},{2,0},{3,1},{4,6},{5,7},{6,4},{7,5},{8,10},{9,11},{10,... | collective-permute-start | bytes 49160 | tf_op jit(solution)/shard_map/ppermute | solution.py:37
  171.2 4.8 %collective-permute-start.13 = (f32[8192]{0:T(1024)S(1)}, f32[8192]{0:T(1024)S(1)}, u32[]{:S(2)}, u32[]{:S(2)}) collective-permute-start(f32[8192]{0:T(1024)S(1)} %maximum_select_fusion.5), channel_id=1, source_target_pairs={{0,4},{1,5},{2,6},{3,7},{4,0},{5,1},{6,2},{7,3},{8,12},{9,13},{10,... | collective-permute-start | bytes 98312 | tf_op jit(solution)/shard_map/ppermute | solution.py:37
  176.1 1.3 collective-permute-start.14
  177.4 5.6 %collective-permute-start.15 = (f32[32768]{0:T(1024)S(1)}, f32[32768]{0:T(1024)S(1)}, u32[]{:S(2)}, u32[]{:S(2)}) collective-permute-start(f32[32768]{0:T(1024)S(1)} %maximum_select_fusion.1), channel_id=1, source_target_pairs={{0,16},{1,17},{2,18},{3,19},{4,20},{5,21},{6,22},{7,23},{8,24},{9,... | collective-permute-start | bytes 393224 | tf_op jit(solution)/shard_map/ppermute | solution.py:37
where the time goes:
time: 249 us
  waiting for transfers between devices  104 us (42%)
  other arithmetic  71.6 us (29%)
  starting transfers between devices  38 us (15%)
  local copies, waits for them, and re-layouts  28.1 us (11%)
  matrix products  4.63 us (2%)
    ppermute x3, waiting for transfers between devices, with_halo(): lax.ppermute(tail, axis, [(i, (i + 1) % count) for i in range(ends)])  59.3 us
    another operation x7, other arithmetic, on_device(): factor = jnp.linalg.cholesky(gram)  34.9 us
    ppermute x10, waiting for transfers between devices, swapped(): return lax.ppermute(value, axis, pairs)  25.2 us
    all_to_all x1, waiting for transfers between devices, on_device(): lax.all_to_all(current, 'band', split_axis=2, concat_axis=0, tiled=True)  19.8 us
    another operation x4, other arithmetic, on_device(): lax.linalg.triangular_solve(factor, flat, left_side=True, lower=True)  19.8 us
    ppermute x10, starting transfers between devices, swapped(): return lax.ppermute(value, axis, pairs)  16.7 us
    ppermute x3, starting transfers between devices, with_halo(): lax.ppermute(tail, axis, [(i, (i + 1) % count) for i in range(ends)])  13.8 us
    unnamed x16, local copies, waits for them, and re-layouts  10.5 us
  transfers between devices with their start and end apart: 17, of which 14 were waited for; matrix products, arithmetic and copies ran while one was open for 1% of the time, Pallas kernels for 0%

commit v1 on v0

--- a/solution.py
+++ b/solution.py
@@ -1,6 +1,10 @@
+import functools
+
 import jax
 import jax.numpy as jnp
 from jax import lax
+from jax.experimental import pallas as pl
+from jax.experimental.pallas import tpu as pltpu
 from jax.sharding import PartitionSpec as P
 
 DEGREE = 3
@@ -31,10 +35,141 @@
     return cells
 
 
-def swapped(value, axis, bit):
-    mask = 2**bit
-    pairs = [(source, source ^ mask) for source in range(lax.axis_size(axis))]
-    return lax.ppermute(value, axis, pairs)
+MESH = pl.DeviceIdType.MESH
+HIGHEST = lax.Precision.HIGHEST
+BLOCK = 64
+TILE = 8
+
+
+def matmul(left, right, dims):
+    return lax.dot_general(
+        left, right, (dims, ((), ())), precision=HIGHEST, preferred_element_type=jnp.float32
+    )
+
+
+def factor_block(diagonal):
+    size = diagonal.shape[0]
+    rows = lax.broadcasted_iota(jnp.int32, (size, size), 0)
+    columns = lax.broadcasted_iota(jnp.int32, (size, size), 1)
+    unit = jnp.where(rows == columns, 1.0, 0.0).astype(jnp.float32)
+    work = jnp.concatenate([diagonal, unit], axis=1)
+    width = work.shape[1]
+    in_tile = lax.broadcasted_iota(jnp.int32, (TILE, width), 0)
+    done = []
+    for start in range(0, size, TILE):
+        count = size - start
+        row_in = lax.broadcasted_iota(jnp.int32, (count, width), 0)
+        panel = [
+            jnp.broadcast_to(work[:, start + k : start + k + 1], (count, width))
+            for k in range(TILE)
+        ]
+        scale = jnp.zeros((TILE, width), jnp.float32)
+        for k in range(TILE):
+            pivot = panel[k][k : k + 1, :]
+            inverse = 1.0 / pivot
+            scale = jnp.where(in_tile == k, 1.0 / jnp.sqrt(pivot), scale)
+            weight = jnp.where(row_in > k, panel[k] * inverse, 0.0)
+            for later in range(k + 1, TILE):
+                panel[later] = panel[later] - weight * panel[later][k : k + 1, :]
+            work = work - weight * work[k : k + 1, :]
+        done.append(work[:TILE] * scale)
+        work = work[TILE:]
+    return jnp.concatenate(done, axis=0)[:, size:]
+
+
+def inverse_factor(work_ref, size):
+    rows = lax.broadcasted_iota(jnp.int32, (size, size), 0)
+    columns = lax.broadcasted_iota(jnp.int32, (size, size), 1)
+    work_ref[:, size:] = jnp.where(rows == columns, 1.0, 0.0).astype(jnp.float32)
+    for first in range(0, size, BLOCK):
+        last = first + BLOCK
+        low = first // 128 * 128
+        high = size + -(-last // 128) * 128
+        small = factor_block(work_ref[first:last, first:last])
+        solved = matmul(small, work_ref[first:last, low:high], ((1,), (0,)))
+        work_ref[first:last, low:high] = solved
+        if last < size:
+            aligned = last // 128 * 128
+            update = matmul(solved[:, aligned - low : size - low], solved, ((0,), (0,)))
+            work_ref[last:, low:high] -= update[last - aligned :]
+
+
+def factor_kernel(axes, cell_total, gram_ref, out_ref, parts, mine, work, send_sems, recv_sems):
+    size = gram_ref.shape[0]
+    if axes:
+        (outer, outer_size), (inner, inner_size) = axes
+        count = outer_size * inner_size
+        share = size // count
+        me = lax.axis_index(outer) * inner_size + lax.axis_index(inner)
+
+        def peer(offset):
+            index = lax.rem(me + offset, count)
+            return index, {outer: index // inner_size, inner: lax.rem(index, inner_size)}
+
+        barrier = pltpu.get_barrier_semaphore()
+        for offset in range(1, count):
+            pl.semaphore_signal(barrier, inc=1, device_id=peer(offset)[1], device_id_type=MESH)
+        pl.semaphore_wait(barrier, count - 1)
+        for offset in range(1, count):
+            index, target = peer(offset)
+            pltpu.make_async_remote_copy(
+                src_ref=gram_ref.at[pl.ds(pl.multiple_of(index * share, share), share)],
+                dst_ref=parts.at[offset - 1],
+                send_sem=send_sems.at[0],
+                recv_sem=recv_sems.at[0],
+                device_id=target,
+                device_id_type=MESH,
+            ).start()
+        own = pl.ds(pl.multiple_of(me * share, share), share)
+        pltpu.make_async_copy(parts, parts, recv_sems.at[0]).wait()
+        mine[...] = (jnp.sum(parts[...], axis=0) + gram_ref[own]) / cell_total
+        for offset in range(1, count):
+            index, target = peer(offset)
+            pltpu.make_async_remote_copy(
+                src_ref=mine,
+                dst_ref=work.at[own, 0:size],
+                send_sem=send_sems.at[1],
+                recv_sem=recv_sems.at[1],
+                device_id=target,
+                device_id_type=MESH,
+            ).start()
+        pltpu.make_async_copy(parts, parts, send_sems.at[0]).wait()
+        others = work.at[0 : size - share, 0:size]
+        pltpu.make_async_copy(others, others, recv_sems.at[1]).wait()
+        work[own, 0:size] = mine[...]
+        pltpu.make_async_copy(parts, parts, send_sems.at[1]).wait()
+    else:
+        work[:, 0:size] = gram_ref[...] / cell_total
+    inverse_factor(work, size)
+    out_ref[...] = work[:, size:]
+
+
+def inverse_of_gram(gram, cell_total):
+    size = gram.shape[0]
+    axes = tuple((name, lax.axis_size(name)) for name in ("band", "space"))
+    count = axes[0][1] * axes[1][1]
+    direct = size % (count * TILE) == 0
+    if not direct:
+        gram = lax.psum(gram, ("band", "space"))
+    share = size // count if direct else TILE
+    peers = count - 1 if direct else 1
+    return pl.pallas_call(
+        functools.partial(factor_kernel, axes if direct else (), float(cell_total)),
+        out_shape=jax.ShapeDtypeStruct((size, size), jnp.float32),
+        in_specs=[pl.BlockSpec(memory_space=pltpu.VMEM)],
+        out_specs=pl.BlockSpec(memory_space=pltpu.VMEM),
+        scratch_shapes=[
+            pltpu.VMEM((peers, share, size), jnp.float32),
+            pltpu.VMEM((share, size), jnp.float32),
+            pltpu.VMEM((size, 2 * size), jnp.float32),
+            pltpu.SemaphoreType.DMA((2,)),
+            pltpu.SemaphoreType.DMA((2,)),
+        ],
+        compiler_params=pltpu.CompilerParams(
+            collective_id=1 if direct else None, has_side_effects=direct
+        ),
+        name="gram_factor",
+    )(gram)
 
 
 def apply_ham(extended, potential, metric, z_weights):
@@ -101,26 +236,10 @@
     local_gram = jnp.dot(
         flat, flat.T, precision=lax.Precision.HIGHEST, preferred_element_type=jnp.float32
     )
-    device_index = lax.axis_index(("band", "space"))
-    levels = lax.axis_size(("band", "space")).bit_length() - 1
-    vector = local_gram.reshape(-1)
-    for level in range(levels):
-        bit = levels - 1 - level
-        half = vector.shape[0] // 2
-        upper_side = device_index >> bit & 1 == 1
-        kept = jnp.where(upper_side, vector[half:], vector[:half])
-        sending = jnp.where(upper_side, vector[:half], vector[half:])
-        vector = kept + swapped(sending, ("band", "space"), bit)
-    for level in range(levels):
-        bit = level
-        upper_side = device_index >> bit & 1 == 1
-        received = swapped(vector, ("band", "space"), bit)
-        vector = jnp.where(
-            upper_side, jnp.concatenate([received, vector]), jnp.concatenate([vector, received])
-        )
-    gram = vector.reshape(all_states, all_states) / cell_total
-    factor = jnp.linalg.cholesky(gram)
-    result = lax.linalg.triangular_solve(factor, flat, left_side=True, lower=True)
+    inverse = inverse_of_gram(local_gram, cell_total)
+    result = jnp.dot(
+        inverse, flat, precision=lax.Precision.HIGHEST, preferred_element_type=jnp.float32
+    )
     return result.reshape(all_states, planes, regrouped.shape[2])
 
 

time: 249 us -> 182 us (0.73)
  other arithmetic: 71.6 us -> 16.4 us
  waiting for transfers between devices: 104 us -> 59.3 us
  Pallas kernels: 0 us -> 37.1 us
  blocking collectives: 0 us -> 22.6 us
  starting transfers between devices: 38 us -> 17.6 us
  local copies, waits for them, and re-layouts: 28.1 us -> 22.3 us
    another operation x11 -> x0, other arithmetic: 54.7 us -> none  [the longest x7 34.9 us: on_device(): factor = jnp.linalg.cholesky(gram)]
    pallas_call x0 -> x1, Pallas kernels: none -> 37.1 us  [inverse_of_gram(): pl.pallas_call(functools.partial(factor_kernel, axes if direct else (), f...]
    ppermute x10 -> x0, waiting for transfers between devices: 25.2 us -> none  [swapped(): return lax.ppermute(value, axis, pairs)]
    all_to_all x0 -> x1, blocking collectives: none -> 22.6 us  [on_device(): lax.all_to_all(current, 'band', split_axis=2, concat_axis=0, tiled=True)]
    all_to_all x1 -> x0, waiting for transfers between devices: 19.8 us -> none  [on_device(): lax.all_to_all(current, 'band', split_axis=2, concat_axis=0, tiled=True)]
    ppermute x10 -> x0, starting transfers between devices: 16.7 us -> none  [swapped(): return lax.ppermute(value, axis, pairs)]
    another operation x11 -> x0, local copies, waits for them, and re-layouts: 4.63 us -> none
    all_to_all x1 -> x0, starting transfers between devices: 3.74 us -> none  [on_device(): lax.all_to_all(current, 'band', split_axis=2, concat_axis=0, tiled=True)]
  transfers between devices with their start and end apart: 17 -> 6, of which waited for: 14 -> 3; matrix products, arithmetic and copies ran while one was open for 1% -> 1% of each run, Pallas kernels for 0% -> 0%
where the time goes in v1:
time: 182 us; the launch traced here: 181 us
  waiting for transfers between devices  59.3 us (33%)
  Pallas kernels  37.1 us (20%)
  blocking collectives  22.6 us (12%)
  local copies, waits for them, and re-layouts  22.3 us (12%)
  starting transfers between devices  17.6 us (10%)
  other arithmetic  16.4 us (9%)
  matrix products  5.98 us (3%)
    ppermute x3, waiting for transfers between devices, with_halo(): lax.ppermute(tail, axis, [(i, (i + 1) % count) for i in range(ends)])  59.3 us
    pallas_call x1, Pallas kernels, inverse_of_gram(): pl.pallas_call(functools.partial(factor_kernel, axes if direct else (), f...  37.1 us
    all_to_all x1, blocking collectives, on_device(): lax.all_to_all(current, 'band', split_axis=2, concat_axis=0, tiled=True)  22.6 us
    ppermute x3, starting transfers between devices, with_halo(): lax.ppermute(tail, axis, [(i, (i + 1) % count) for i in range(ends)])  13.8 us
    unnamed x12, local copies, waits for them, and re-layouts  10.6 us
    sub x2, other arithmetic, on_device(): following = 2.0 * (applied - CENTRE * current) / HALF_WIDTH - earlier  7.6 us
    all_to_all x1, other arithmetic, on_device(): lax.all_to_all(current, 'band', split_axis=2, concat_axis=0, tiled=True)  5.21 us
    all_to_all x2, local copies, waits for them, and re-layouts, on_device(): lax.all_to_all(current, 'band', split_axis=2, concat_axis=0, tiled=True)  4.45 us
  transfers between devices with their start and end apart: 6, of which 3 were waited for; matrix products, arithmetic and copies ran while one was open for 1% of the time, Pallas kernels for 0%

profile of v1, /device:TPU:0, one launch (start us, length us, event | category | flops | bytes accessed | tf_op | source)
XLA Modules:
  0.0 181.5 jit_solution(7058698591984709594)
XLA Ops:
  0.0 0.0 copy-start
  0.0 0.0 copy-start.3
  0.0 2.3 %fusion.135 = (f32[64,2,1024]{2,0,1:T(8,128)}, f32[64,2,1024]{2,0,1:T(8,128)}) fusion(f32[64,6,1024]{2,0,1:T(8,128)} %param.4), kind=kLoop, calls=%fused_computation.187 | loop fusion | bytes 2097152 | tf_op jit(solution)/shard_map/slice | solution.py:26
  2.3 0.0 copy-start.1
  2.3 5.0 %collective-permute-start = (f32[64,2,1024]{2,0,1:T(8,128)}, f32[64,2,1024]{2,0,1:T(8,128)S(1)}, u32[]{:S(2)}, u32[]{:S(2)}) collective-permute-start(f32[64,2,1024]{2,0,1:T(8,128)} %get-tuple-element.16), channel_id=1, source_target_pairs={{0,1},{1,2},{2,3},{3,4},{4,5},{5,6},{6,7},{8,9},{9,10},{10,11},{11... | collective-permute-start | bytes 1572872 | tf_op jit(solution)/shard_map/ppermute | solution.py:29
  7.3 1.3 collective-permute-start.1
  8.6 0.0 copy-done
  8.6 0.0 copy-done.3
  8.6 0.2 fusion.102
  8.9 0.2 reshape.59
  9.1 0.8 slice_reduce_fusion.2
  9.9 0.1 mul.364
  10.0 0.1 mul.372
  10.1 0.1 mul.379
  10.3 19.7 %collective-permute-done = f32[64,2,1024]{2,0,1:T(8,128)S(1)} collective-permute-done((f32[64,2,1024]{2,0,1:T(8,128)}, f32[64,2,1024]{2,0,1:T(8,128)S(1)}, u32[]{:S(2)}, u32[]{:S(2)}) %collective-permute-start) | collective-permute-done | bytes 524320 | tf_op jit(solution)/shard_map/ppermute | solution.py:29
  30.0 0.0 copy-done.1
  30.1 0.0 copy-start.2
  30.1 0.2 constant_dynamic-update-slice_fusion
  30.3 0.0 collective-permute-done.1
  30.4 0.5 copy-done.2
  30.8 3.6 %broadcast_multiply_fusion = (f32[64,6,1024]{2,0,1:T(8,128)S(1)}, f32[64,6,1024]{2,0,1:T(8,128)S(1)}) fusion(f32[64,6,1024]{2,0,1:T(8,128)S(1)} %copy-done.1, f32[1024]{0:T(1024)S(1)} %get-tuple-element.18, f32[1024]{0:T(1024)S(1)} %get-tuple-element.19, f32[1024]{0:T(1024)S(1)} %fusion.130, f32[1024]{0:T(1024)S(1)} %get-tuple-element.20, ...), kind=kLoop, calls=%fused_computation.140 | loop fusion | flops 14548992 | bytes 11128832 | tf_op jit(solution)/shard_map/div | solution.py:226
  34.4 0.1 fusion.134
  34.5 4.3 %collective-permute-start.2 = (f32[64,2,1024]{2,0,1:T(8,128)S(1)}, f32[64,2,1024]{2,0,1:T(8,128)S(1)}, u32[]{:S(2)}, u32[]{:S(2)}) collective-permute-start(f32[64,2,1024]{2,0,1:T(8,128)S(1)} %get-tuple-element.12), channel_id=1, source_target_pairs={{0,1},{1,2},{2,3},{3,4},{4,5},{5,6},{6,7},{8,9},{9,10},{10,11},{11... | collective-permute-start | bytes 1572872 | tf_op jit(solution)/shard_map/ppermute | solution.py:29
  38.8 1.3 collective-permute-start.3
  40.1 20.2 %collective-permute-done.2 = f32[64,2,1024]{2,0,1:T(8,128)S(1)} collective-permute-done((f32[64,2,1024]{2,0,1:T(8,128)S(1)}, f32[64,2,1024]{2,0,1:T(8,128)S(1)}, u32[]{:S(2)}, u32[]{:S(2)}) %collective-permute-start.2) | collective-permute-done | bytes 524320 | tf_op jit(solution)/shard_map/ppermute | solution.py:29
  60.3 0.0 collective-permute-done.3
  60.3 3.8 %fusion.35 = f32[64,6,1024]{2,0,1:T(8,128)S(1)} fusion(f32[64,6,1024]{2,0,1:T(8,128)S(1)} %copy-done.1, f32[64,6,1024]{2,0,1:T(8,128)S(1)} %get-tuple-element.8, f32[64,2,1024]{2,0,1:T(8,128)S(1)} %collective-permute-done.3, f32[64,2,1024]{2,0,1:T(8,128)S(1)} %collective-permute-done.2, f32[64,6,1024]{2,0,1:T(8,128)S(1)} %get-tuple-element.9, ...), kind=kLoop, calls=%fused_computation.67 | loop fusion | flops 16515072 | bytes 7458816 | tf_op jit(solution)/shard_map/sub | solution.py:229
  64.1 0.1 fusion.133
  64.3 4.4 %collective-permute-start.4 = (f32[64,2,1024]{2,0,1:T(8,128)S(1)}, f32[64,2,1024]{2,0,1:T(8,128)S(1)}, u32[]{:S(2)}, u32[]{:S(2)}) collective-permute-start(f32[64,2,1024]{2,0,1:T(8,128)S(1)} %get-tuple-element.10), channel_id=1, source_target_pairs={{0,1},{1,2},{2,3},{3,4},{4,5},{5,6},{6,7},{8,9},{9,10},{10,11},{11... | collective-permute-start | bytes 1572872 | tf_op jit(solution)/shard_map/ppermute | solution.py:29
  68.7 1.3 collective-permute-start.5
  70.0 19.4 %collective-permute-done.4 = f32[64,2,1024]{2,0,1:T(8,128)S(1)} collective-permute-done((f32[64,2,1024]{2,0,1:T(8,128)S(1)}, f32[64,2,1024]{2,0,1:T(8,128)S(1)}, u32[]{:S(2)}, u32[]{:S(2)}) %collective-permute-start.4) | collective-permute-done | bytes 524320 | tf_op jit(solution)/shard_map/ppermute | solution.py:29
  89.3 0.0 collective-permute-done.5
  89.3 3.8 %fusion.60 = f32[64,6,1024]{2,0,1:T(8,128)S(1)} fusion(f32[64,6,1024]{2,0,1:T(8,128)S(1)} %fusion.35, f32[64,2,1024]{2,0,1:T(8,128)S(1)} %collective-permute-done.5, f32[64,2,1024]{2,0,1:T(8,128)S(1)} %collective-permute-done.4, f32[64,6,1024]{2,0,1:T(8,128)S(1)} %get-tuple-element.9, f32[1024]{0:T(1024)S(1)} %get-tuple-element.18, ...), kind=kLoop, calls=%fused_computation.92 | loop fusion | flops 16908288 | bytes 5885952 | tf_op jit(solution)/shard_map/sub | solution.py:229
  93.1 2.7 %copy.25 = f32[64,6,1024]{0,1,2:T(8,128)} copy(f32[64,6,1024]{2,0,1:T(8,128)S(1)} %fusion.60) | data formatting | bytes 3145728 | tf_op jit(solution)/shard_map/sub | solution.py:229
  95.8 4.2 %reshape.80 = f32[4,1,98304]{2,1,0:T(1,128)S(1)} reshape(f32[1024,6,64]{2,1,0:T(8,128)} %bitcast.22) | data formatting | bytes 3145728
  100.1 22.6 %all_to_all.15 = f32[4,1,98304]{2,1,0:T(1,128)S(1)} all-to-all(f32[4,1,98304]{2,1,0:T(1,128)S(1)} %reshape.80), channel_id=1, replica_groups=mesh['band'=4,'space'=8] {'band'}, dimensions={0} | all-to-all | bytes 3145728 | tf_op jit(solution)/shard_map/all_to_all | solution.py:232
  122.7 0.5 broadcast.289
  123.2 5.2 %reduce.12 = f32[4,98304]{1,0:T(4,128)S(1)} reduce(f32[4,1,98304]{2,1,0:T(1,128)S(1)} %all_to_all.15, f32[]{:T(128)} %broadcast.289), dimensions={1}, to_apply=%all_to_all.11.reduce_sub_computation | reduce | bytes 3145732 | tf_op jit(solution)/shard_map/all_to_all | solution.py:232
  128.4 3.6 %reshape.81 = f32[1024,6,64]{2,1,0:T(8,128)} reshape(f32[4,98304]{1,0:T(4,128)S(1)} %reduce.12) | data formatting | bytes 3145728
  132.0 3.9 %copy.26 = f32[64,6,4,256]{3,1,0,2:T(8,128)} copy(f32[64,6,4,256]{0,1,3,2:T(8,128)} %bitcast.23) | data formatting | bytes 3145728 | tf_op jit(solution)/shard_map/all_to_all | solution.py:232
  136.0 2.3 %copy.28 = f32[32,8,6,256]{3,1,2,0:T(8,128)S(1)} copy(f32[32,8,6,256]{3,2,1,0:T(8,128)} %bitcast.24) | data formatting | bytes 3145728
  138.2 0.5 copy.27
  138.7 2.2 %fusion.136.gram_ref = f32[256,256]{1,0:T(8,128)} fusion(f32[256,1536]{1,0:T(8,128)S(1)} %bitcast.21), kind=kOutput, calls=%fused_computation.188 | convolution fusion | flops 1207959552 | bytes 1835008 | tf_op jit(solution)/shard_map/dot_general | solution.py:236
  140.8 37.1 %gram_factor.1 = f32[256,256]{1,0:T(8,128)} custom-call(f32[256,256]{1,0:T(8,128)} %fusion.136.gram_ref), custom_call_target="tpu_custom_call" | custom-call | tf_op jit(solution)/shard_map/gram_factor/pallas_call | solution.py:156
  177.9 3.6 %fusion.100 = f32[256,6,256]{2,0,1:T(8,128)} fusion(f32[6,256,256]{2,1,0:T(8,128)S(1)} %bitcast.25, f32[256,256]{1,0:T(8,128)} %gram_factor.1), kind=kOutput, calls=%fused_computation.141 | convolution fusion | flops 1207959552 | bytes 3407872 | tf_op jit(solution)/shard_map/dot_general | solution.py:240
  (7 shorter events, 0.1 us)
Async XLA Ops:
  0.0 8.6 %copy-start = (f32[64,96]{1,0:T(8,128)S(1)}, f32[64,96]{1,0:T(8,128)}, u32[]{:S(2)}) copy-start(f32[64,96]{1,0:T(8,128)} %param.6) | copy-start | bytes 73732
  0.0 8.6 %copy-start.3 = (s32[6,32]{1,0:T(8,128)S(1)}, s32[6,32]{1,0:T(8,128)}, u32[]{:S(2)}) copy-start(s32[6,32]{1,0:T(8,128)} %param.5) | copy-start | bytes 2308
  2.3 27.8 %copy-start.1 = (f32[64,6,1024]{2,0,1:T(8,128)S(1)}, f32[64,6,1024]{2,0,1:T(8,128)}, u32[]{:S(2)}) copy-start(f32[64,6,1024]{2,0,1:T(8,128)} %param.4) | copy-start | bytes 4718596
  2.3 27.7 %collective-permute-start = (f32[64,2,1024]{2,0,1:T(8,128)}, f32[64,2,1024]{2,0,1:T(8,128)S(1)}, u32[]{:S(2)}, u32[]{:S(2)}) collective-permute-start(f32[64,2,1024]{2,0,1:T(8,128)} %get-tuple-element.16), channel_id=1, source_target_pairs={{0,1},{1,2},{2,3},{3,4},{4,5},{5,6},{6,7},{8,9},{9,10},{10,11},{11... | collective-permute-start | bytes 1572872 | tf_op jit(solution)/shard_map/ppermute | solution.py:29
  7.3 23.0 %collective-permute-start.1 = (f32[64,2,1024]{2,0,1:T(8,128)}, f32[64,2,1024]{2,0,1:T(8,128)S(1)}, u32[]{:S(2)}, u32[]{:S(2)}) collective-permute-start(f32[64,2,1024]{2,0,1:T(8,128)} %get-tuple-element.17), channel_id=1, source_target_pairs={{1,0},{2,1},{3,2},{4,3},{5,4},{6,5},{7,6},{9,8},{10,9},{11,10},{12... | collective-permute-start | bytes 1572872 | tf_op jit(solution)/shard_map/ppermute | solution.py:31
  30.1 0.8 copy-start.2
  34.5 25.8 %collective-permute-start.2 = (f32[64,2,1024]{2,0,1:T(8,128)S(1)}, f32[64,2,1024]{2,0,1:T(8,128)S(1)}, u32[]{:S(2)}, u32[]{:S(2)}) collective-permute-start(f32[64,2,1024]{2,0,1:T(8,128)S(1)} %get-tuple-element.12), channel_id=1, source_target_pairs={{0,1},{1,2},{2,3},{3,4},{4,5},{5,6},{6,7},{8,9},{9,10},{10,11},{11... | collective-permute-start | bytes 1572872 | tf_op jit(solution)/shard_map/ppermute | solution.py:29
  38.8 21.5 %collective-permute-start.3 = (f32[64,2,1024]{2,0,1:T(8,128)S(1)}, f32[64,2,1024]{2,0,1:T(8,128)S(1)}, u32[]{:S(2)}, u32[]{:S(2)}) collective-permute-start(f32[64,2,1024]{2,0,1:T(8,128)S(1)} %get-tuple-element.13), channel_id=1, source_target_pairs={{1,0},{2,1},{3,2},{4,3},{5,4},{6,5},{7,6},{9,8},{10,9},{11,10},{12... | collective-permute-start | bytes 1572872 | tf_op jit(solution)/shard_map/ppermute | solution.py:31
  64.3 25.1 %collective-permute-start.4 = (f32[64,2,1024]{2,0,1:T(8,128)S(1)}, f32[64,2,1024]{2,0,1:T(8,128)S(1)}, u32[]{:S(2)}, u32[]{:S(2)}) collective-permute-start(f32[64,2,1024]{2,0,1:T(8,128)S(1)} %get-tuple-element.10), channel_id=1, source_target_pairs={{0,1},{1,2},{2,3},{3,4},{4,5},{5,6},{6,7},{8,9},{9,10},{10,11},{11... | collective-permute-start | bytes 1572872 | tf_op jit(solution)/shard_map/ppermute | solution.py:29
  68.7 20.7 %collective-permute-start.5 = (f32[64,2,1024]{2,0,1:T(8,128)S(1)}, f32[64,2,1024]{2,0,1:T(8,128)S(1)}, u32[]{:S(2)}, u32[]{:S(2)}) collective-permute-start(f32[64,2,1024]{2,0,1:T(8,128)S(1)} %get-tuple-element.11), channel_id=1, source_target_pairs={{1,0},{2,1},{3,2},{4,3},{5,4},{6,5},{7,6},{9,8},{10,9},{11,10},{12... | collective-permute-start | bytes 1572872 | tf_op jit(solution)/shard_map/ppermute | solution.py:31

commit v2 on v1

--- a/solution.py
+++ b/solution.py
@@ -16,23 +16,6 @@
 HALF_WIDTH = 7.5
 OFFSETS = (-2, -1, 0, 1, 2)
 WEIGHTS = (-1.0 / 12.0, 4.0 / 3.0, -2.5, 4.0 / 3.0, -1.0 / 12.0)
-
-
-def with_halo(cells, sides, width):
-    for axis, dim in sides:
-        count = lax.axis_size(axis)
-        ends = count - 1
-        head = lax.slice_in_dim(cells, 0, width, axis=dim)
-        tail = lax.slice_in_dim(cells, cells.shape[dim] - width, cells.shape[dim], axis=dim)
-        cells = jnp.concatenate(
-            [
-                lax.ppermute(tail, axis, [(i, (i + 1) % count) for i in range(ends)]),
-                cells,
-                lax.ppermute(head, axis, [((i + 1) % count, i) for i in range(ends)]),
-            ],
-            axis=dim,
-        )
-    return cells
 
 
 MESH = pl.DeviceIdType.MESH
@@ -172,75 +155,293 @@
     )(gram)
 
 
-def apply_ham(extended, potential, metric, z_weights):
-    planes = extended.shape[1] - 4
-    plane_cells = extended.shape[2]
-    block = extended[:, 2 : 2 + planes, :]
-    row_pad = 2 * NZ
-    padded = jnp.pad(block, ((0, 0), (0, 0), (row_pad, row_pad)))
-    x_term = WEIGHTS[0] * extended[:, 2 + OFFSETS[0] : 2 + OFFSETS[0] + planes, :]
-    y_term = (
-        WEIGHTS[0]
-        * padded[:, :, row_pad + OFFSETS[0] * NZ : row_pad + OFFSETS[0] * NZ + plane_cells]
-    )
-    z_term = z_weights[0] * padded[:, :, row_pad + OFFSETS[0] : row_pad + OFFSETS[0] + plane_cells]
-    for position in range(1, 5):
-        offset = OFFSETS[position]
-        weight = WEIGHTS[position]
-        x_term = x_term + weight * extended[:, 2 + offset : 2 + offset + planes, :]
-        y_term = (
-            y_term
-            + weight * padded[:, :, row_pad + offset * NZ : row_pad + offset * NZ + plane_cells]
+FIRST = 4.0 / 3.0
+SECOND = -1.0 / 12.0
+REACH = 2
+
+
+def order_of(chunks, steps):
+    pairs = [(chunk, step) for chunk in range(chunks) for step in range(steps)]
+    return sorted(pairs, key=lambda pair: (pair[0] + pair[1], -pair[1]))
+
+
+def filter_kernel(
+    bands, spaces, states, base, shift_weights, out, grids, last, cells, base_sems,
+    in_send, in_recv, own_sems, halo_send, halo_recv, out_send, out_recv,
+):
+    planes, held, plane_cells = states.shape
+    half = held // 2
+    chunks = half // TILE
+    both = 2 * planes
+    share = plane_cells // bands
+    band = lax.axis_index("band")
+    space = lax.axis_index("space")
+    side = lax.rem(space, 2)
+    partner = space + 1 - 2 * side
+    ends = {0: space >= 2, 1: space < spaces - 2}
+    towards = {0: space - 2, 1: space + 2}
+
+    def to(target_band, target_space):
+        return {"band": target_band, "space": target_space}
+
+    barrier = pltpu.get_barrier_semaphore()
+    for turn in range(bands):
+        target = lax.rem(band + turn, bands)
+        if turn:
+            pl.semaphore_signal(
+                barrier, inc=1, device_id=to(target, space), device_id_type=MESH
+            )
+        pl.semaphore_signal(barrier, inc=1, device_id=to(target, partner), device_id_type=MESH)
+    for end in (0, 1):
+
+        @pl.when(ends[end])
+        def _():
+            pl.semaphore_signal(
+                barrier, inc=1, device_id=to(band, towards[end]), device_id_type=MESH
+            )
+
+    below = jnp.minimum(space // 2, 1)
+    above = jnp.minimum((spaces - 1 - space) // 2, 1)
+    pl.semaphore_wait(barrier, 2 * bands - 1 + below + above)
+
+    own_planes = pl.ds(REACH + side * planes, planes)
+    base_out = pltpu.make_async_remote_copy(
+        src_ref=base,
+        dst_ref=cells.at[side],
+        send_sem=base_sems.at[0],
+        recv_sem=base_sems.at[1],
+        device_id=to(band, partner),
+        device_id_type=MESH,
+    )
+    base_own = pltpu.make_async_copy(base, cells.at[side], base_sems.at[2])
+    enter, keep = [], []
+    for chunk in range(chunks):
+        given = pl.ds(pl.multiple_of((1 - side) * half + chunk * TILE, TILE), TILE)
+        kept = pl.ds(pl.multiple_of(side * half + chunk * TILE, TILE), TILE)
+        enter.append(
+            pltpu.make_async_remote_copy(
+                src_ref=states.at[:, given],
+                dst_ref=grids.at[0, chunk, own_planes],
+                send_sem=in_send.at[chunk],
+                recv_sem=in_recv.at[chunk],
+                device_id=to(band, partner),
+                device_id_type=MESH,
+            )
         )
-        z_term = (
-            z_term
-            + z_weights[position] * padded[:, :, row_pad + offset : row_pad + offset + plane_cells]
+        keep.append(
+            pltpu.make_async_copy(
+                states.at[:, kept], grids.at[0, chunk, own_planes], own_sems.at[chunk]
+            )
         )
-    kinetic = metric[0] * x_term + metric[1] * y_term + metric[2] * z_term
-    return potential * block - 0.5 * kinetic
-
-
-def on_device(states, patch_ids, metric_table, potential):
-    planes = states.shape[1]
-    plane_cells = states.shape[2]
+    enter[0].start()
+    base_out.start()
+    base_own.start()
+    keep[0].start()
+    for chunk in range(1, chunks):
+        enter[chunk].start()
+        keep[chunk].start()
+
+    for end in (0, 1):
+
+        @pl.when(jnp.logical_not(ends[end]))
+        def _():
+            edge = end * (both + REACH)
+            for step in range(DEGREE):
+                for chunk in range(chunks):
+                    grids[step, chunk, edge : edge + REACH] = jnp.zeros(
+                        (REACH, TILE, plane_cells), jnp.float32
+                    )
+
+    def halo(step, chunk, end):
+        source = REACH if end == 0 else both
+        landing = both + REACH if end == 0 else 0
+        return pltpu.make_async_remote_copy(
+            src_ref=grids.at[step, chunk, source : source + REACH],
+            dst_ref=grids.at[step, chunk, landing : landing + REACH],
+            send_sem=halo_send.at[step, chunk, end],
+            recv_sem=halo_recv.at[step, chunk, end],
+            device_id=to(band, towards[end]),
+            device_id_type=MESH,
+        )
+
+    def landed(step, chunk, end):
+        landing = 0 if end == 0 else both + REACH
+        return pltpu.make_async_copy(
+            grids.at[step, chunk, landing : landing + REACH],
+            grids.at[step, chunk, landing : landing + REACH],
+            halo_recv.at[step, chunk, 1 - end],
+        )
+
+    def send_halos(step, chunk):
+        for end in (0, 1):
+
+            @pl.when(ends[end])
+            def _():
+                halo(step, chunk, end).start()
+
+    def apply(step, chunk):
+        def plane(index, carry):
+            here = REACH + index
+            slab = index // planes
+            row = pl.ds(index - slab * planes, 1)
+            value = grids[step, chunk, here]
+            near = grids[step, chunk, here - 1] + grids[step, chunk, here + 1]
+            far = grids[step, chunk, here - 2] + grids[step, chunk, here + 2]
+            total = cells[slab, 0, row] * value
+            total = total + cells[slab, 1, row] * (FIRST * near + SECOND * far)
+            for kind, stride in ((0, NZ), (1, 1)):
+                part = None
+                for position, offset in enumerate((-2, -1, 1, 2)):
+                    amount = (-offset * stride) % plane_cells
+                    moved = pltpu.roll(value, amount, axis=1)
+                    number = kind * 4 + position
+                    term = shift_weights[number : number + 1] * moved
+                    part = term if part is None else part + term
+                total = total + cells[slab, 2 + kind, row] * part
+            if step > 0:
+                total = 2.0 * total - grids[step - 1, chunk, here]
+            if step < DEGREE - 1:
+                grids[step + 1, chunk, here] = total
+            else:
+                last[chunk, index] = total
+            return carry
+
+        lax.fori_loop(0, both, plane, 0)
+
+    def leave(chunk):
+        rows = pl.ds(pl.multiple_of(band * held + side * half + chunk * TILE, TILE), TILE)
+        for turn in range(bands):
+            target = lax.rem(band + turn, bands)
+            columns = pl.ds(pl.multiple_of(target * share, share), share)
+            for other in (1, 0):
+                slab = side if other == 0 else 1 - side
+                source = last.at[chunk, pl.ds(slab * planes, planes), :, columns]
+                landing = out.at[:, rows, :]
+                if turn == 0 and other == 0:
+                    pltpu.make_async_copy(source, landing, out_recv.at[0]).start()
+                else:
+                    pltpu.make_async_remote_copy(
+                        src_ref=source,
+                        dst_ref=landing,
+                        send_sem=out_send.at[0],
+                        recv_sem=out_recv.at[0],
+                        device_id=to(target, space if other == 0 else partner),
+                        device_id_type=MESH,
+                    ).start()
+
+    for chunk, step in order_of(chunks, DEGREE):
+        if step == 0:
+            if chunk == 0:
+                base_own.wait()
+                base_out.wait_recv()
+            keep[chunk].wait()
+            enter[chunk].wait_recv()
+            send_halos(0, chunk)
+        for end in (0, 1):
+
+            @pl.when(ends[end])
+            def _():
+                landed(step, chunk, end).wait()
+
+        apply(step, chunk)
+        if step < DEGREE - 1:
+            send_halos(step + 1, chunk)
+        else:
+            leave(chunk)
+
+    base_out.wait_send()
+    for chunk in range(chunks):
+        enter[chunk].wait_send()
+        for step in range(DEGREE):
+            for end in (0, 1):
+
+                @pl.when(ends[end])
+                def _():
+                    halo(step, chunk, end).wait_send()
+
+    pltpu.make_async_copy(out, out, out_recv.at[0]).wait()
+    sent = out.at[:, 0 : out.shape[1] - out.shape[1] // (2 * bands), :]
+    pltpu.make_async_copy(sent, sent, out_send.at[0]).wait()
+
+
+def filtered_and_regrouped(states, base, shift_weights):
+    planes, held, plane_cells = states.shape
+    bands = lax.axis_size("band")
+    spaces = lax.axis_size("space")
+    chunks = held // 2 // TILE
+    both = 2 * planes
+    dma = pltpu.SemaphoreType.DMA
+    return pl.pallas_call(
+        functools.partial(filter_kernel, bands, spaces),
+        out_shape=jax.ShapeDtypeStruct((planes, held * bands, plane_cells // bands), jnp.float32),
+        in_specs=[
+            pl.BlockSpec(memory_space=pl.ANY),
+            pl.BlockSpec(memory_space=pltpu.VMEM),
+            pl.BlockSpec(memory_space=pltpu.VMEM),
+        ],
+        out_specs=pl.BlockSpec(memory_space=pl.ANY),
+        scratch_shapes=[
+            pltpu.VMEM((DEGREE, chunks, both + 2 * REACH, TILE, plane_cells), jnp.float32),
+            pltpu.VMEM((chunks, both, TILE, plane_cells), jnp.float32),
+            pltpu.VMEM((2,) + base.shape, jnp.float32),
+            dma((3,)),
+            dma((chunks,)),
+            dma((chunks,)),
+            dma((chunks,)),
+            dma((DEGREE, chunks, 2)),
+            dma((DEGREE, chunks, 2)),
+            dma((1,)),
+            dma((1,)),
+        ],
+        compiler_params=pltpu.CompilerParams(
+            collective_id=0, has_side_effects=True, vmem_limit_bytes=40 * 2**20
+        ),
+        name="filter_regroup",
+    )(states, base, shift_weights)
+
+
+def coefficients(patch_ids, metric_table, potential):
+    planes, plane_cells = potential.shape
     one_hot = (patch_ids[:, :, None] == jnp.arange(metric_table.shape[0], dtype=jnp.int32)).astype(
         jnp.float32
     )
-    looked = jnp.einsum("xyp,pm->xym", one_hot, metric_table, precision=lax.Precision.HIGHEST)
+    looked = jnp.einsum("xyp,pm->xym", one_hot, metric_table, precision=HIGHEST)
     metric = looked.reshape(planes, NY, 3, NZ).transpose(2, 0, 1, 3).reshape(3, planes, plane_cells)
-    z_index = jnp.arange(plane_cells, dtype=jnp.int32) % NZ
-    z_weights = [
-        WEIGHTS[position]
-        * ((z_index + OFFSETS[position] >= 0) & (z_index + OFFSETS[position] < NZ)).astype(
-            jnp.float32
+    kinetic = metric * (-0.5 / HALF_WIDTH)
+    centre = (potential - CENTRE) / HALF_WIDTH + WEIGHTS[2] * (
+        kinetic[0] + kinetic[1] + kinetic[2]
+    )
+    base = jnp.concatenate([centre[None], kinetic], axis=0)
+    return jnp.pad(base, ((0, 0), (0, -planes % TILE), (0, 0)))
+
+
+def on_device(states, patch_ids, metric_table, potential):
+    planes, plane_cells = potential.shape
+    index = jnp.arange(plane_cells, dtype=jnp.int32)
+    rows = []
+    for place in (index // NZ, index % NZ):
+        length = NY if not rows else NZ
+        for offset, weight in ((-2, SECOND), (-1, FIRST), (1, FIRST), (2, SECOND)):
+            inside = (place + offset >= 0) & (place + offset < length)
+            rows.append(jnp.where(inside, weight, 0.0).astype(jnp.float32))
+    shift_weights = jnp.stack(rows)
+    base = coefficients(patch_ids, metric_table, potential)
+    filtered = filtered_and_regrouped(states.transpose(1, 0, 2), base, shift_weights)
+    cell_total = planes * plane_cells * lax.axis_size("space")
+    local_gram = lax.dot_general(
+        filtered[0], filtered[0], (((1,), (1,)), ((), ())), precision=HIGHEST,
+        preferred_element_type=jnp.float32,
+    )
+    for plane in range(1, planes):
+        local_gram = local_gram + lax.dot_general(
+            filtered[plane], filtered[plane], (((1,), (1,)), ((), ())), precision=HIGHEST,
+            preferred_element_type=jnp.float32,
         )
-        for position in range(5)
-    ]
-
-    def step_ham(block):
-        extended = with_halo(block, (("space", 1),), 2)
-        return apply_ham(extended, potential, metric, z_weights)
-
-    applied = step_ham(states)
-    earlier = states
-    current = (applied - CENTRE * states) / HALF_WIDTH
-    for degree_step in range(DEGREE - 1):
-        applied = step_ham(current)
-        following = 2.0 * (applied - CENTRE * current) / HALF_WIDTH - earlier
-        earlier = current
-        current = following
-    regrouped = lax.all_to_all(current, "band", split_axis=2, concat_axis=0, tiled=True)
-    all_states = regrouped.shape[0]
-    flat = regrouped.reshape(all_states, -1)
-    cell_total = planes * plane_cells * lax.axis_size("space")
-    local_gram = jnp.dot(
-        flat, flat.T, precision=lax.Precision.HIGHEST, preferred_element_type=jnp.float32
-    )
     inverse = inverse_of_gram(local_gram, cell_total)
-    result = jnp.dot(
-        inverse, flat, precision=lax.Precision.HIGHEST, preferred_element_type=jnp.float32
-    )
-    return result.reshape(all_states, planes, regrouped.shape[2])
+    result = jnp.einsum(
+        "ts,psc->ptc", inverse, filtered, precision=HIGHEST, preferred_element_type=jnp.float32
+    )
+    return result.transpose(1, 0, 2)
 
 
 def solution(mesh):

time: 182 us -> 107 us (0.59)
  Pallas kernels: 37.1 us -> 97.3 us
  waiting for transfers between devices: 59.3 us -> 0 us
  blocking collectives: 22.6 us -> 0 us
  local copies, waits for them, and re-layouts: 22.3 us -> 1.14 us
  starting transfers between devices: 17.6 us -> 0 us
  other arithmetic: 16.4 us -> 0.51 us
    pallas_call x0 -> x1, Pallas kernels: none -> 67.4 us  [filtered_and_regrouped(): pl.pallas_call(functools.partial(filter_kernel, bands, spaces), out_shape...]
    ppermute x6 -> x0, waiting for transfers between devices: 59.3 us -> none  [the longest x3 59.3 us: with_halo(): lax.ppermute(tail, axis, [(i, (i + 1) % count) for i in range(ends)])]
    all_to_all x1 -> x0, blocking collectives: 22.6 us -> none  [on_device(): lax.all_to_all(current, 'band', split_axis=2, concat_axis=0, tiled=True)]
    ppermute x6 -> x0, starting transfers between devices: 17.6 us -> none  [the longest x3 13.8 us: with_halo(): lax.ppermute(tail, axis, [(i, (i + 1) % count) for i in range(ends)])]
    unnamed x12 -> x6, local copies, waits for them, and re-layouts: 10.6 us -> 0.61 us
    sub x2 -> x0, other arithmetic: 7.6 us -> none  [on_device(): following = 2.0 * (applied - CENTRE * current) / HALF_WIDTH - earlier]
    pallas_call x1, Pallas kernels: 37.1 us -> 29.9 us  [inverse_of_gram(): pl.pallas_call(functools.partial(factor_kernel, axes if direct else (), f...]
    all_to_all x1 -> x0, other arithmetic: 5.21 us -> none  [on_device(): lax.all_to_all(current, 'band', split_axis=2, concat_axis=0, tiled=True)]
  transfers between devices with their start and end apart: 6 -> 0, of which waited for: 3 -> 0; matrix products, arithmetic and copies ran while one was open for 1% -> 0% of each run, Pallas kernels for 0% -> 0%
where the time goes in v2:
time: 107 us
  Pallas kernels  97.3 us (91%)
  matrix products  7.65 us (7%)
  local copies, waits for them, and re-layouts  1.14 us (1%)
    pallas_call x1, Pallas kernels, filtered_and_regrouped(): pl.pallas_call(functools.partial(filter_kernel, bands, spaces), out_shape...  67.4 us
    pallas_call x1, Pallas kernels, inverse_of_gram(): pl.pallas_call(functools.partial(factor_kernel, axes if direct else (), f...  29.9 us
    dot_general x1, matrix products, on_device(): jnp.einsum('ts,psc->ptc', inverse, filtered, precision=HIGHEST, preferred...  3.54 us
    dot_general x5, matrix products, on_device(): lax.dot_general(filtered[plane], filtered[plane], (((1,), (1,)), ((), ())...  2.77 us

profile of v2, /device:TPU:0, one launch (start us, length us, event | category | flops | bytes accessed | tf_op | source)
XLA Modules:
  0.0 106.8 jit_solution(3409143241401677607)
XLA Ops:
  0.0 0.0 copy-start
  0.0 0.0 copy-start.2
  0.0 0.0 copy-start.1
  0.1 0.1 stack.2.shift_weights
  0.2 0.6 copy-done
  0.8 0.9 convolution_multiply_fusion
  1.7 0.2 mul.26
  1.9 0.4 fusion.16
  2.3 0.2 mul.31
  2.5 0.1 mul.30
  2.6 0.0 copy-done.2
  2.7 0.0 copy-done.1
  2.7 67.4 %filter_regroup.1 = f32[6,256,256]{2,1,0:T(8,128)S(1)} custom-call(f32[6,64,1024]{2,1,0:T(8,128)S(1)} %bitcast.31, f32[4,8,1024]{2,1,0:T(8,128)S(1)} %select_maximum_fusion.base, f32[8,1024]{1,0:T(8,128)S(1)} %stack.2.shift_weights), custom_call_target="tpu_custom_call" | custom-call | tf_op jit(solution)/shard_map/filter_regroup/pallas_call | solution.py:374
  70.1 0.4 fusion.7
  70.5 0.4 convolution_add_fusion.4
  70.9 0.4 convolution_add_fusion.3
  71.3 0.4 convolution_add_fusion.2
  71.7 0.4 convolution_add_fusion.1
  72.2 1.1 %convolution_add_fusion.gram_ref = f32[256,256]{1,0:T(8,128)} fusion(f32[256,256]{1,0:T(8,128)S(1)} %convolution_add_fusion.1, f32[6,256,256]{2,1,0:T(8,128)S(1)} %filter_regroup.1), kind=kOutput, calls=%fused_computation | convolution fusion | flops 201392128 | bytes 786432 | tf_op jit(solution)/shard_map/dot_general | solution.py:436
  73.3 29.9 %gram_factor.1 = f32[256,256]{1,0:T(8,128)} custom-call(f32[256,256]{1,0:T(8,128)} %convolution_add_fusion.gram_ref), custom_call_target="tpu_custom_call" | custom-call | tf_op jit(solution)/shard_map/gram_factor/pallas_call | solution.py:139
  103.2 3.5 %fusion = f32[256,6,256]{2,0,1:T(8,128)} fusion(f32[6,256,256]{2,1,0:T(8,128)S(1)} %filter_regroup.1, f32[256,256]{1,0:T(8,128)} %gram_factor.1), kind=kOutput, calls=%fused_computation.6 | convolution fusion | flops 1207959552 | bytes 3407872 | tf_op jit(solution)/shard_map/ts,psc->ptc/dot_general | solution.py:441
  (7 shorter events, 0.1 us)
Async XLA Ops:
  0.0 0.8 copy-start
  0.0 2.6 %copy-start.2 = (f32[6,1024]{1,0:T(8,128)S(1)}, f32[6,1024]{1,0:T(8,128)}, u32[]{:S(2)}) copy-start(f32[6,1024]{1,0:T(8,128)} %param.7) | copy-start | bytes 73732
  0.0 2.6 %copy-start.1 = (f32[64,6,1024]{2,0,1:T(8,128)S(1)}, f32[64,6,1024]{2,0,1:T(8,128)}, u32[]{:S(2)}) copy-start(f32[64,6,1024]{2,0,1:T(8,128)} %param.4) | copy-start | bytes 4718596

commit v3 on v2

--- a/solution.py
+++ b/solution.py
@@ -160,26 +160,25 @@
 REACH = 2
 
 
-def order_of(chunks, steps):
-    pairs = [(chunk, step) for chunk in range(chunks) for step in range(steps)]
-    return sorted(pairs, key=lambda pair: (pair[0] + pair[1], -pair[1]))
-
-
 def filter_kernel(
-    bands, spaces, states, base, shift_weights, out, grids, last, cells, base_sems,
-    in_send, in_recv, own_sems, halo_send, halo_recv, out_send, out_recv,
+    bands, spaces, states, base, shift_weights, out, grids, last, cells, base_send, base_recv,
+    in_send, in_recv, keep_sems, halo_send, halo_recv, out_send, out_recv,
 ):
     planes, held, plane_cells = states.shape
     half = held // 2
     chunks = half // TILE
-    both = 2 * planes
+    span = 4 * planes
     share = plane_cells // bands
     band = lax.axis_index("band")
     space = lax.axis_index("space")
     side = lax.rem(space, 2)
     partner = space + 1 - 2 * side
+    outward = space + 4 * side - 2
+    across = space - 4 * side + 2
     ends = {0: space >= 2, 1: space < spaces - 2}
     towards = {0: space - 2, 1: space + 2}
+    has_outward = jnp.logical_and(outward >= 0, outward < spaces)
+    has_across = jnp.logical_and(across >= 0, across < spaces)
 
     def to(target_band, target_space):
         return {"band": target_band, "space": target_space}
@@ -204,91 +203,89 @@
     above = jnp.minimum((spaces - 1 - space) // 2, 1)
     pl.semaphore_wait(barrier, 2 * bands - 1 + below + above)
 
-    own_planes = pl.ds(REACH + side * planes, planes)
-    base_out = pltpu.make_async_remote_copy(
-        src_ref=base,
-        dst_ref=cells.at[side],
-        send_sem=base_sems.at[0],
-        recv_sem=base_sems.at[1],
-        device_id=to(band, partner),
-        device_id_type=MESH,
-    )
-    base_own = pltpu.make_async_copy(base, cells.at[side], base_sems.at[2])
-    enter, keep = [], []
+    def slab(place):
+        return pl.ds(place * planes, planes)
+
+    def rows_of(part, chunk):
+        return pl.ds(pl.multiple_of(part * half + chunk * TILE, TILE), TILE)
+
+    def remote(source, landing, send_sem, recv_sem, target):
+        return pltpu.make_async_remote_copy(
+            src_ref=source,
+            dst_ref=landing,
+            send_sem=send_sem,
+            recv_sem=recv_sem,
+            device_id=to(band, target),
+            device_id_type=MESH,
+        )
+
+    own, theirs = 1 + side, 2 - side
+    own_landing, passed_landing = 3 * (1 - side), 3 * side
+    base_sends = (
+        remote(base, cells.at[own], base_send.at[0], base_recv.at[0], partner),
+        remote(base, cells.at[own_landing], base_send.at[1], base_recv.at[1], outward),
+        remote(cells.at[theirs], cells.at[passed_landing], base_send.at[2], base_recv.at[2], across),
+    )
+    base_keep = pltpu.make_async_copy(base, cells.at[own], base_send.at[3])
+    enter, keep, halo_own, halo_passed = [], [], [], []
     for chunk in range(chunks):
-        given = pl.ds(pl.multiple_of((1 - side) * half + chunk * TILE, TILE), TILE)
-        kept = pl.ds(pl.multiple_of(side * half + chunk * TILE, TILE), TILE)
+        grid = grids.at[0, chunk]
+        kept = states.at[:, rows_of(side, chunk)]
         enter.append(
-            pltpu.make_async_remote_copy(
-                src_ref=states.at[:, given],
-                dst_ref=grids.at[0, chunk, own_planes],
-                send_sem=in_send.at[chunk],
-                recv_sem=in_recv.at[chunk],
-                device_id=to(band, partner),
-                device_id_type=MESH,
+            remote(
+                states.at[:, rows_of(1 - side, chunk)], grid.at[slab(own)],
+                in_send.at[chunk], in_recv.at[chunk], partner,
             )
         )
-        keep.append(
-            pltpu.make_async_copy(
-                states.at[:, kept], grids.at[0, chunk, own_planes], own_sems.at[chunk]
+        keep.append(pltpu.make_async_copy(kept, grid.at[slab(own)], keep_sems.at[chunk]))
+        halo_own.append(
+            remote(
+                kept, grid.at[slab(own_landing)],
+                halo_send.at[0, chunk], halo_recv.at[0, chunk], outward,
             )
         )
-    enter[0].start()
-    base_out.start()
-    base_own.start()
-    keep[0].start()
-    for chunk in range(1, chunks):
+        halo_passed.append(
+            remote(
+                grid.at[slab(theirs)], grid.at[slab(passed_landing)],
+                halo_send.at[1, chunk], halo_recv.at[1, chunk], across,
+            )
+        )
+
+    def begin(chunk):
         enter[chunk].start()
+
+        @pl.when(has_outward)
+        def _():
+            if chunk == 0:
+                base_sends[1].start()
+            halo_own[chunk].start()
+
+    base_sends[0].start()
+    base_keep.start()
+    for chunk in range(chunks):
         keep[chunk].start()
-
-    for end in (0, 1):
-
-        @pl.when(jnp.logical_not(ends[end]))
-        def _():
-            edge = end * (both + REACH)
-            for step in range(DEGREE):
-                for chunk in range(chunks):
-                    grids[step, chunk, edge : edge + REACH] = jnp.zeros(
-                        (REACH, TILE, plane_cells), jnp.float32
-                    )
-
-    def halo(step, chunk, end):
-        source = REACH if end == 0 else both
-        landing = both + REACH if end == 0 else 0
-        return pltpu.make_async_remote_copy(
-            src_ref=grids.at[step, chunk, source : source + REACH],
-            dst_ref=grids.at[step, chunk, landing : landing + REACH],
-            send_sem=halo_send.at[step, chunk, end],
-            recv_sem=halo_recv.at[step, chunk, end],
-            device_id=to(band, towards[end]),
-            device_id_type=MESH,
-        )
-
-    def landed(step, chunk, end):
-        landing = 0 if end == 0 else both + REACH
-        return pltpu.make_async_copy(
-            grids.at[step, chunk, landing : landing + REACH],
-            grids.at[step, chunk, landing : landing + REACH],
-            halo_recv.at[step, chunk, 1 - end],
-        )
-
-    def send_halos(step, chunk):
-        for end in (0, 1):
-
-            @pl.when(ends[end])
-            def _():
-                halo(step, chunk, end).start()
+    for chunk in range(min(2, chunks)):
+        begin(chunk)
+
+    for place, missing in ((0, space < 2), (3, space >= spaces - 2)):
+
+        @pl.when(missing)
+        def _():
+            cells[place] = jnp.zeros(cells.shape[1:], jnp.float32)
+            for chunk in range(chunks):
+                for plane in range(place * planes, (place + 1) * planes):
+                    grids[0, chunk, plane] = jnp.zeros((TILE, plane_cells), jnp.float32)
 
     def apply(step, chunk):
         def plane(index, carry):
-            here = REACH + index
-            slab = index // planes
-            row = pl.ds(index - slab * planes, 1)
+            here = index
+            place = index // planes
+            row = pl.ds(index - place * planes, 1)
             value = grids[step, chunk, here]
             near = grids[step, chunk, here - 1] + grids[step, chunk, here + 1]
             far = grids[step, chunk, here - 2] + grids[step, chunk, here + 2]
-            total = cells[slab, 0, row] * value
-            total = total + cells[slab, 1, row] * (FIRST * near + SECOND * far)
+            total = cells[place, 0, row] * value
+            total = total + cells[place, 1, row] * (FIRST * near + SECOND * far)
             for kind, stride in ((0, NZ), (1, 1)):
                 part = None
                 for position, offset in enumerate((-2, -1, 1, 2)):
@@ -297,16 +294,17 @@
                     number = kind * 4 + position
                     term = shift_weights[number : number + 1] * moved
                     part = term if part is None else part + term
-                total = total + cells[slab, 2 + kind, row] * part
+                total = total + cells[place, 2 + kind, row] * part
             if step > 0:
                 total = 2.0 * total - grids[step - 1, chunk, here]
             if step < DEGREE - 1:
                 grids[step + 1, chunk, here] = total
             else:
-                last[chunk, index] = total
+                last[chunk, index - planes] = total
             return carry
 
-        lax.fori_loop(0, both, plane, 0)
+        edge = REACH * (step + 1)
+        lax.fori_loop(edge, span - edge, plane, 0)
 
     def leave(chunk):
         rows = pl.ds(pl.multiple_of(band * held + side * half + chunk * TILE, TILE), TILE)
@@ -314,8 +312,7 @@
             target = lax.rem(band + turn, bands)
             columns = pl.ds(pl.multiple_of(target * share, share), share)
             for other in (1, 0):
-                slab = side if other == 0 else 1 - side
-                source = last.at[chunk, pl.ds(slab * planes, planes), :, columns]
+                source = last.at[chunk, slab(side if other == 0 else 1 - side), :, columns]
                 landing = out.at[:, rows, :]
                 if turn == 0 and other == 0:
                     pltpu.make_async_copy(source, landing, out_recv.at[0]).start()
@@ -329,35 +326,57 @@
                         device_id_type=MESH,
                     ).start()
 
-    for chunk, step in order_of(chunks, DEGREE):
-        if step == 0:
+    def finish(chunk):
+        @pl.when(has_across)
+        def _():
             if chunk == 0:
-                base_own.wait()
-                base_out.wait_recv()
-            keep[chunk].wait()
-            enter[chunk].wait_recv()
-            send_halos(0, chunk)
-        for end in (0, 1):
-
-            @pl.when(ends[end])
-            def _():
-                landed(step, chunk, end).wait()
-
-        apply(step, chunk)
-        if step < DEGREE - 1:
-            send_halos(step + 1, chunk)
-        else:
-            leave(chunk)
-
-    base_out.wait_send()
+                base_sends[1].wait_recv()
+            halo_own[chunk].wait_recv()
+
+        @pl.when(has_outward)
+        def _():
+            if chunk == 0:
+                base_sends[2].wait_recv()
+            halo_passed[chunk].wait_recv()
+
+        for step in range(DEGREE):
+            apply(step, chunk)
+        leave(chunk)
+
+    for chunk in range(chunks):
+        if chunk == 0:
+            base_keep.wait()
+            base_sends[0].wait_recv()
+        keep[chunk].wait()
+        enter[chunk].wait_recv()
+
+        @pl.when(has_across)
+        def _():
+            if chunk == 0:
+                base_sends[2].start()
+            halo_passed[chunk].start()
+
+        if chunk + 2 < chunks:
+            begin(chunk + 2)
+        if chunk > 0:
+            finish(chunk - 1)
+    finish(chunks - 1)
+
+    base_sends[0].wait_send()
     for chunk in range(chunks):
         enter[chunk].wait_send()
-        for step in range(DEGREE):
-            for end in (0, 1):
-
-                @pl.when(ends[end])
-                def _():
-                    halo(step, chunk, end).wait_send()
+
+    @pl.when(has_outward)
+    def _():
+        base_sends[1].wait_send()
+        for chunk in range(chunks):
+            halo_own[chunk].wait_send()
+
+    @pl.when(has_across)
+    def _():
+        base_sends[2].wait_send()
+        for chunk in range(chunks):
+            halo_passed[chunk].wait_send()
 
     pltpu.make_async_copy(out, out, out_recv.at[0]).wait()
     sent = out.at[:, 0 : out.shape[1] - out.shape[1] // (2 * bands), :]
@@ -369,7 +388,8 @@
     bands = lax.axis_size("band")
     spaces = lax.axis_size("space")
     chunks = held // 2 // TILE
-    both = 2 * planes
+    if planes != REACH * DEGREE:
+        raise ValueError("slab depth")
     dma = pltpu.SemaphoreType.DMA
     return pl.pallas_call(
         functools.partial(filter_kernel, bands, spaces),
@@ -381,15 +401,16 @@
         ],
         out_specs=pl.BlockSpec(memory_space=pl.ANY),
         scratch_shapes=[
-            pltpu.VMEM((DEGREE, chunks, both + 2 * REACH, TILE, plane_cells), jnp.float32),
-            pltpu.VMEM((chunks, both, TILE, plane_cells), jnp.float32),
-            pltpu.VMEM((2,) + base.shape, jnp.float32),
+            pltpu.VMEM((DEGREE, chunks, 4 * planes, TILE, plane_cells), jnp.float32),
+            pltpu.VMEM((chunks, 2 * planes, TILE, plane_cells), jnp.float32),
+            pltpu.VMEM((4,) + base.shape, jnp.float32),
+            dma((4,)),
             dma((3,)),
             dma((chunks,)),
             dma((chunks,)),
             dma((chunks,)),
-            dma((DEGREE, chunks, 2)),
-            dma((DEGREE, chunks, 2)),
+            dma((2, chunks)),
+            dma((2, chunks)),
             dma((1,)),
             dma((1,)),
         ],

time: 107 us -> 93.7 us (0.88)
  Pallas kernels: 97.3 us -> 84.1 us
    pallas_call x1, Pallas kernels: 67.4 us -> 53.9 us  [filtered_and_regrouped(): pl.pallas_call(functools.partial(filter_kernel, bands, spaces), out_shape...]
where the time goes in v3:
time: 93.7 us; the launch traced here: 93.5 us
  Pallas kernels  84.1 us (90%)
  matrix products  7.65 us (8%)
  local copies, waits for them, and re-layouts  1.14 us (1%)
    pallas_call x1, Pallas kernels, filtered_and_regrouped(): pl.pallas_call(functools.partial(filter_kernel, bands, spaces), out_shape...  53.9 us
    pallas_call x1, Pallas kernels, inverse_of_gram(): pl.pallas_call(functools.partial(factor_kernel, axes if direct else (), f...  30.2 us
    dot_general x1, matrix products, on_device(): jnp.einsum('ts,psc->ptc', inverse, filtered, precision=HIGHEST, preferred...  3.54 us
    dot_general x5, matrix products, on_device(): lax.dot_general(filtered[plane], filtered[plane], (((1,), (1,)), ((), ())...  2.77 us

profile of v3, /device:TPU:0, one launch (start us, length us, event | category | flops | bytes accessed | tf_op | source)
XLA Modules:
  0.0 93.5 jit_solution(5705407372778388718)
XLA Ops:
  0.0 0.0 copy-start
  0.0 0.0 copy-start.2
  0.0 0.0 copy-start.1
  0.1 0.1 stack.2.shift_weights
  0.2 0.6 copy-done
  0.8 0.9 convolution_multiply_fusion
  1.7 0.2 mul.26
  1.9 0.4 fusion.16
  2.3 0.2 mul.31
  2.5 0.1 mul.30
  2.6 0.0 copy-done.2
  2.7 0.0 copy-done.1
  2.7 53.9 %filter_regroup.1 = f32[6,256,256]{2,1,0:T(8,128)S(1)} custom-call(f32[6,64,1024]{2,1,0:T(8,128)S(1)} %bitcast.31, f32[4,8,1024]{2,1,0:T(8,128)S(1)} %select_maximum_fusion.base, f32[8,1024]{1,0:T(8,128)S(1)} %stack.2.shift_weights), custom_call_target="tpu_custom_call" | custom-call | tf_op jit(solution)/shard_map/filter_regroup/pallas_call | solution.py:394
  56.6 0.4 fusion.7
  57.0 0.4 convolution_add_fusion.4
  57.4 0.4 convolution_add_fusion.3
  57.8 0.4 convolution_add_fusion.2
  58.3 0.4 convolution_add_fusion.1
  58.7 1.1 %convolution_add_fusion.gram_ref = f32[256,256]{1,0:T(8,128)} fusion(f32[256,256]{1,0:T(8,128)S(1)} %convolution_add_fusion.1, f32[6,256,256]{2,1,0:T(8,128)S(1)} %filter_regroup.1), kind=kOutput, calls=%fused_computation | convolution fusion | flops 201392128 | bytes 786432 | tf_op jit(solution)/shard_map/dot_general | solution.py:457
  59.8 30.2 %gram_factor.1 = f32[256,256]{1,0:T(8,128)} custom-call(f32[256,256]{1,0:T(8,128)} %convolution_add_fusion.gram_ref), custom_call_target="tpu_custom_call" | custom-call | tf_op jit(solution)/shard_map/gram_factor/pallas_call | solution.py:139
  90.0 3.5 %fusion = f32[256,6,256]{2,0,1:T(8,128)} fusion(f32[6,256,256]{2,1,0:T(8,128)S(1)} %filter_regroup.1, f32[256,256]{1,0:T(8,128)} %gram_factor.1), kind=kOutput, calls=%fused_computation.6 | convolution fusion | flops 1207959552 | bytes 3407872 | tf_op jit(solution)/shard_map/ts,psc->ptc/dot_general | solution.py:462
  (7 shorter events, 0.1 us)
Async XLA Ops:
  0.0 0.8 copy-start
  0.0 2.6 %copy-start.2 = (f32[6,1024]{1,0:T(8,128)S(1)}, f32[6,1024]{1,0:T(8,128)}, u32[]{:S(2)}) copy-start(f32[6,1024]{1,0:T(8,128)} %param.7) | copy-start | bytes 73732
  0.0 2.6 %copy-start.1 = (f32[64,6,1024]{2,0,1:T(8,128)S(1)}, f32[64,6,1024]{2,0,1:T(8,128)}, u32[]{:S(2)}) copy-start(f32[64,6,1024]{2,0,1:T(8,128)} %param.4) | copy-start | bytes 4718596

commit v4 on v3

--- a/solution.py
+++ b/solution.py
@@ -77,50 +77,64 @@
             work_ref[last:, low:high] -= update[last - aligned :]
 
 
-def factor_kernel(axes, cell_total, gram_ref, out_ref, parts, mine, work, send_sems, recv_sems):
+def factor_kernel(
+    bands, spaces, cell_total, gram_ref, out_ref, near, far, mine, final, work, send_sems, recv_sems
+):
     size = gram_ref.shape[0]
-    if axes:
-        (outer, outer_size), (inner, inner_size) = axes
-        count = outer_size * inner_size
-        share = size // count
-        me = lax.axis_index(outer) * inner_size + lax.axis_index(inner)
-
-        def peer(offset):
-            index = lax.rem(me + offset, count)
-            return index, {outer: index // inner_size, inner: lax.rem(index, inner_size)}
-
-        barrier = pltpu.get_barrier_semaphore()
-        for offset in range(1, count):
-            pl.semaphore_signal(barrier, inc=1, device_id=peer(offset)[1], device_id_type=MESH)
-        pl.semaphore_wait(barrier, count - 1)
-        for offset in range(1, count):
-            index, target = peer(offset)
+    if bands:
+        near_count, far_count = 2 * bands, spaces // 2
+        share = size // near_count
+        band, space = lax.axis_index("band"), lax.axis_index("space")
+        line = space // 2
+        side = space - 2 * line
+        place = 2 * band + side
+        own = pl.ds(pl.multiple_of(place * share, share), share)
+
+        def near_peer(offset):
+            index = lax.rem(place + offset, near_count)
+            return index, {"band": index // 2, "space": 2 * line + lax.rem(index, 2)}
+
+        def far_peer(offset):
+            return {"band": band, "space": 2 * lax.rem(line + offset, far_count) + side}
+
+        def send(source, landing, stage, target):
             pltpu.make_async_remote_copy(
-                src_ref=gram_ref.at[pl.ds(pl.multiple_of(index * share, share), share)],
-                dst_ref=parts.at[offset - 1],
-                send_sem=send_sems.at[0],
-                recv_sem=recv_sems.at[0],
+                src_ref=source,
+                dst_ref=landing,
+                send_sem=send_sems.at[stage],
+                recv_sem=recv_sems.at[stage],
                 device_id=target,
                 device_id_type=MESH,
             ).start()
-        own = pl.ds(pl.multiple_of(me * share, share), share)
-        pltpu.make_async_copy(parts, parts, recv_sems.at[0]).wait()
-        mine[...] = (jnp.sum(parts[...], axis=0) + gram_ref[own]) / cell_total
-        for offset in range(1, count):
-            index, target = peer(offset)
-            pltpu.make_async_remote_copy(
-                src_ref=mine,
-                dst_ref=work.at[own, 0:size],
-                send_sem=send_sems.at[1],
-                recv_sem=recv_sems.at[1],
-                device_id=target,
-                device_id_type=MESH,
-            ).start()
-        pltpu.make_async_copy(parts, parts, send_sems.at[0]).wait()
-        others = work.at[0 : size - share, 0:size]
+
+        barrier = pltpu.get_barrier_semaphore()
+        for offset in range(1, near_count):
+            pl.semaphore_signal(
+                barrier, inc=1, device_id=near_peer(offset)[1], device_id_type=MESH
+            )
+        for offset in range(1, far_count):
+            pl.semaphore_signal(barrier, inc=1, device_id=far_peer(offset), device_id_type=MESH)
+        pl.semaphore_wait(barrier, near_count + far_count - 2)
+        for offset in range(1, near_count):
+            index, target = near_peer(offset)
+            rows = pl.ds(pl.multiple_of(index * share, share), share)
+            send(gram_ref.at[rows], near.at[offset - 1], 0, target)
+        pltpu.make_async_copy(near, near, recv_sems.at[0]).wait()
+        mine[...] = jnp.sum(near[...], axis=0) + gram_ref[own]
+        for offset in range(1, far_count):
+            send(mine, far.at[line], 1, far_peer(offset))
+        others = far.at[0 : far_count - 1]
         pltpu.make_async_copy(others, others, recv_sems.at[1]).wait()
-        work[own, 0:size] = mine[...]
-        pltpu.make_async_copy(parts, parts, send_sems.at[1]).wait()
+        far[line] = mine[...]
+        final[...] = jnp.sum(far[...], axis=0) / cell_total
+        for offset in range(1, near_count):
+            send(final, work.at[own, 0:size], 2, near_peer(offset)[1])
+        rest = work.at[0 : size - share, 0:size]
+        pltpu.make_async_copy(rest, rest, recv_sems.at[2]).wait()
+        work[own, 0:size] = final[...]
+        pltpu.make_async_copy(near, near, send_sems.at[0]).wait()
+        pltpu.make_async_copy(others, others, send_sems.at[1]).wait()
+        pltpu.make_async_copy(near, near, send_sems.at[2]).wait()
     else:
         work[:, 0:size] = gram_ref[...] / cell_total
     inverse_factor(work, size)
@@ -129,24 +143,26 @@
 
 def inverse_of_gram(gram, cell_total):
     size = gram.shape[0]
-    axes = tuple((name, lax.axis_size(name)) for name in ("band", "space"))
-    count = axes[0][1] * axes[1][1]
-    direct = size % (count * TILE) == 0
+    bands, spaces = lax.axis_size("band"), lax.axis_size("space")
+    direct = size % (2 * bands * TILE) == 0 and spaces % 2 == 0 and spaces >= 4
     if not direct:
         gram = lax.psum(gram, ("band", "space"))
-    share = size // count if direct else TILE
-    peers = count - 1 if direct else 1
+        bands, spaces = 0, 4
+    near_count = 2 * max(bands, 1)
+    share = size // near_count
     return pl.pallas_call(
-        functools.partial(factor_kernel, axes if direct else (), float(cell_total)),
+        functools.partial(factor_kernel, bands, spaces, float(cell_total)),
         out_shape=jax.ShapeDtypeStruct((size, size), jnp.float32),
         in_specs=[pl.BlockSpec(memory_space=pltpu.VMEM)],
         out_specs=pl.BlockSpec(memory_space=pltpu.VMEM),
         scratch_shapes=[
-            pltpu.VMEM((peers, share, size), jnp.float32),
+            pltpu.VMEM((near_count - 1, share, size), jnp.float32),
+            pltpu.VMEM((spaces // 2, share, size), jnp.float32),
+            pltpu.VMEM((share, size), jnp.float32),
             pltpu.VMEM((share, size), jnp.float32),
             pltpu.VMEM((size, 2 * size), jnp.float32),
-            pltpu.SemaphoreType.DMA((2,)),
-            pltpu.SemaphoreType.DMA((2,)),
+            pltpu.SemaphoreType.DMA((3,)),
+            pltpu.SemaphoreType.DMA((3,)),
         ],
         compiler_params=pltpu.CompilerParams(
             collective_id=1 if direct else None, has_side_effects=direct
@@ -277,13 +293,14 @@
                     grids[0, chunk, plane] = jnp.zeros((TILE, plane_cells), jnp.float32)
 
     def apply(step, chunk):
-        def plane(index, carry):
-            here = index
-            place = index // planes
-            row = pl.ds(index - place * planes, 1)
-            value = grids[step, chunk, here]
-            near = grids[step, chunk, here - 1] + grids[step, chunk, here + 1]
-            far = grids[step, chunk, here - 2] + grids[step, chunk, here + 2]
+        edge = REACH * (step + 1)
+
+        def stencil(here, around):
+            place = here // planes
+            row = pl.ds(here - place * planes, 1)
+            value = around[2]
+            near = around[1] + around[3]
+            far = around[0] + around[4]
             total = cells[place, 0, row] * value
             total = total + cells[place, 1, row] * (FIRST * near + SECOND * far)
             for kind, stride in ((0, NZ), (1, 1)):
@@ -297,14 +314,20 @@
                 total = total + cells[place, 2 + kind, row] * part
             if step > 0:
                 total = 2.0 * total - grids[step - 1, chunk, here]
-            if step < DEGREE - 1:
-                grids[step + 1, chunk, here] = total
-            else:
-                last[chunk, index - planes] = total
+            return total
+
+        def two_planes(pair, carry):
+            first = edge + 2 * pair
+            around = [grids[step, chunk, first + shift] for shift in range(-2, 4)]
+            totals = [stencil(first, around[:5]), stencil(first + 1, around[1:])]
+            for shift, total in enumerate(totals):
+                if step < DEGREE - 1:
+                    grids[step + 1, chunk, first + shift] = total
+                else:
+                    last[chunk, first + shift - planes] = total
             return carry
 
-        edge = REACH * (step + 1)
-        lax.fori_loop(edge, span - edge, plane, 0)
+        lax.fori_loop(0, span // 2 - edge, two_planes, 0)
 
     def leave(chunk):
         rows = pl.ds(pl.multiple_of(band * held + side * half + chunk * TILE, TILE), TILE)

time: 93.7 us -> 85.1 us (0.908)
  Pallas kernels: 84.1 us -> 75.5 us
    pallas_call x1, Pallas kernels: 53.9 us -> 49.6 us  [filtered_and_regrouped(): pl.pallas_call(functools.partial(filter_kernel, bands, spaces), out_shape...]
    pallas_call x1, Pallas kernels: 30.2 us -> 25.9 us  [inverse_of_gram(): pl.pallas_call(functools.partial(factor_kernel, bands, spaces, float(cell...]
where the time goes in v4:
time: 85.1 us; the launch traced here: 84.9 us
  Pallas kernels  75.5 us (89%)
  matrix products  7.65 us (9%)
  local copies, waits for them, and re-layouts  1.14 us (1%)
    pallas_call x1, Pallas kernels, filtered_and_regrouped(): pl.pallas_call(functools.partial(filter_kernel, bands, spaces), out_shape...  49.6 us
    pallas_call x1, Pallas kernels, inverse_of_gram(): pl.pallas_call(functools.partial(factor_kernel, bands, spaces, float(cell...  25.9 us
    dot_general x1, matrix products, on_device(): jnp.einsum('ts,psc->ptc', inverse, filtered, precision=HIGHEST, preferred...  3.54 us
    dot_general x5, matrix products, on_device(): lax.dot_general(filtered[plane], filtered[plane], (((1,), (1,)), ((), ())...  2.77 us

profile of v4, /device:TPU:0, one launch (start us, length us, event | category | flops | bytes accessed | tf_op | source)
XLA Modules:
  0.0 84.9 jit_solution(6429231010500577865)
XLA Ops:
  0.0 0.0 copy-start
  0.0 0.0 copy-start.2
  0.0 0.0 copy-start.1
  0.1 0.1 stack.2.shift_weights
  0.2 0.6 copy-done
  0.8 0.9 %convolution_multiply_fusion = f32[6,32,96]{2,1,0:T(8,128)S(1)} fusion(s32[6,32]{1,0:T(8,128)} %param.5, f32[64,96]{1,0:T(8,128)S(1)} %copy-done), kind=kOutput, calls=%fused_computation.5 | convolution fusion | flops 14186496 | bytes 99072 | tf_op jit(solution)/shard_map/xyp,pm->xym/dot_general | solution.py:452
  1.7 0.2 mul.26
  1.9 0.4 fusion.16
  2.3 0.2 mul.31
  2.5 0.1 mul.30
  2.6 0.0 copy-done.2
  2.7 0.0 copy-done.1
  2.7 49.6 %filter_regroup.1 = f32[6,256,256]{2,1,0:T(8,128)S(1)} custom-call(f32[6,64,1024]{2,1,0:T(8,128)S(1)} %bitcast.31, f32[4,8,1024]{2,1,0:T(8,128)S(1)} %select_maximum_fusion.base, f32[8,1024]{1,0:T(8,128)S(1)} %stack.2.shift_weights), custom_call_target="tpu_custom_call" | custom-call | tf_op jit(solution)/shard_map/filter_regroup/pallas_call | solution.py:417
  52.3 0.4 fusion.7
  52.7 0.4 convolution_add_fusion.4
  53.1 0.4 convolution_add_fusion.3
  53.5 0.4 convolution_add_fusion.2
  53.9 0.4 convolution_add_fusion.1
  54.4 1.1 %convolution_add_fusion.gram_ref = f32[256,256]{1,0:T(8,128)} fusion(f32[256,256]{1,0:T(8,128)S(1)} %convolution_add_fusion.1, f32[6,256,256]{2,1,0:T(8,128)S(1)} %filter_regroup.1), kind=kOutput, calls=%fused_computation | convolution fusion | flops 201392128 | bytes 786432 | tf_op jit(solution)/shard_map/dot_general | solution.py:480
  55.5 25.9 %gram_factor.1 = f32[256,256]{1,0:T(8,128)} custom-call(f32[256,256]{1,0:T(8,128)} %convolution_add_fusion.gram_ref), custom_call_target="tpu_custom_call" | custom-call | tf_op jit(solution)/shard_map/gram_factor/pallas_call | solution.py:153
  81.4 3.5 %fusion = f32[256,6,256]{2,0,1:T(8,128)} fusion(f32[6,256,256]{2,1,0:T(8,128)S(1)} %filter_regroup.1, f32[256,256]{1,0:T(8,128)} %gram_factor.1), kind=kOutput, calls=%fused_computation.6 | convolution fusion | flops 1207959552 | bytes 3407872 | tf_op jit(solution)/shard_map/ts,psc->ptc/dot_general | solution.py:485
  (7 shorter events, 0.1 us)
Async XLA Ops:
  0.0 0.8 copy-start
  0.0 2.6 %copy-start.2 = (f32[6,1024]{1,0:T(8,128)S(1)}, f32[6,1024]{1,0:T(8,128)}, u32[]{:S(2)}) copy-start(f32[6,1024]{1,0:T(8,128)} %param.7) | copy-start | bytes 73732
  0.0 2.6 %copy-start.1 = (f32[64,6,1024]{2,0,1:T(8,128)S(1)}, f32[64,6,1024]{2,0,1:T(8,128)}, u32[]{:S(2)}) copy-start(f32[64,6,1024]{2,0,1:T(8,128)} %param.4) | copy-start | bytes 4718596
